TPU v7x, 32 devices: a whole 2x2x4 slice. The times are simulated.
32 devices in a mesh: src: 2 (over core), brick: 16 (over z, y, x).
Axes of the slice: x: 2, y: 2, z: 4, core: 2. Of those that a mesh axis runs over, the one named last changes fastest.
Arguments:
- slowness: float32 [64, 64, 128], P('brick'), may hold values from 0.5 to 2
- source_x: int32 [4], P('src'), may hold values from 0 to 63
- source_y: int32 [4], P('src'), may hold values from 0 to 63
- source_z: int32 [4], P('src'), may hold values from 0 to 127
- station_x: int32 [2048], replicated, may hold values from 0 to 63
- station_y: int32 [2048], replicated, may hold values from 0 to 63
- station_z: int32 [2048], replicated, may hold values from 0 to 127
- observed: float32 [4, 2048], P('src'), may hold values from 0 to 4
Outputs:
- kernel: float32 [64, 64, 128], P('brick', 'src')
- arrivals: float32 [4, 2048], P('src', 'brick')
All inputs are finite; a program needn't handle non-finite values.
Results may differ from a plain program's by a relative error of at most 0.0003.
Values sent between devices are 32-bit elements; how exact they have to be, the bound alone decides.
A program may use at most 128 MiB of HBM per device.

v0:
```python
import jax
import jax.numpy as jnp
from jax import lax
from jax.sharding import PartitionSpec as P

ITERS = 16


spacing = 0.015625
big_value = 1000000.0
start_slowness = 2.0


def extended(cells, sides, width):
    for axis, dim in sides:
        count = lax.axis_size(axis)
        ends = count - 1
        head = lax.slice_in_dim(cells, 0, width, axis=dim)
        tail = lax.slice_in_dim(cells, cells.shape[dim] - width, cells.shape[dim], axis=dim)
        cells = jnp.concatenate(
            [
                lax.ppermute(tail, axis, [(i, (i + 1) % count) for i in range(ends)]),
                cells,
                lax.ppermute(head, axis, [((i + 1) % count, i) for i in range(ends)]),
            ],
            axis=dim,
        )
    return cells


def neighbours(padded):
    return [
        padded[:, 2:, 1:-1, 1:-1],
        padded[:, :-2, 1:-1, 1:-1],
        padded[:, 1:-1, 2:, 1:-1],
        padded[:, 1:-1, :-2, 1:-1],
        padded[:, 1:-1, 1:-1, 2:],
        padded[:, 1:-1, 1:-1, :-2],
    ]


def per_device(slowness, source_x, source_y, source_z, station_x, station_y, station_z, observed):
    slabs = lax.axis_size("brick")
    slab_id = lax.axis_index("brick")
    cells_x, cells_y, cells_z = slowness.shape
    count = source_x.shape[0]
    grid_x = cells_x * slabs
    width = 2
    extent = cells_x + 2 * width
    first = slab_id * cells_x - width
    ext_x = first + jnp.arange(extent, dtype=jnp.int32)
    outside = ((ext_x < 0) | (ext_x >= grid_x))[None, :, None, None]
    slow_ext = extended(slowness, (("brick", 0),), width)[None]
    slow_pad = jnp.pad(slow_ext, ((0, 0), (1, 1), (1, 1), (1, 1)), constant_values=1.0)
    costs = [spacing * 0.5 * (slow_ext + other) for other in neighbours(slow_pad)]
    own_x = (slab_id * cells_x + jnp.arange(cells_x, dtype=jnp.int32)).astype(jnp.float32)
    pos_y = jnp.arange(cells_y, dtype=jnp.float32)[None, None, :, None]
    pos_z = jnp.arange(cells_z, dtype=jnp.float32)[None, None, None, :]
    dist = (
        (own_x[None, :, None, None] - source_x.astype(jnp.float32)[:, None, None, None]) ** 2
        + (pos_y - source_y.astype(jnp.float32)[:, None, None, None]) ** 2
        + (pos_z - source_z.astype(jnp.float32)[:, None, None, None]) ** 2
    )
    times = start_slowness * spacing * jnp.sqrt(dist)

    def forward_group(group, times):
        field = extended(times, (("brick", 1),), width)
        field = jnp.where(outside, big_value, field)
        for inner in range(width):
            padded = jnp.pad(field, ((0, 0), (1, 1), (1, 1), (1, 1)), constant_values=big_value)
            fresh = field
            for cost, other in zip(costs, neighbours(padded)):
                fresh = jnp.minimum(fresh, other + cost)
            field = jnp.where(outside, big_value, fresh)
        return field[:, width : width + cells_x]

    times = lax.fori_loop(0, ITERS // width, forward_group, times)
    times_ext = extended(times, (("brick", 1),), width)
    times_ext = jnp.where(outside, -big_value, times_ext)
    local_x = station_x - first
    inside_ext = (local_x >= 0) & (local_x < extent)
    owned = (local_x >= width) & (local_x < width + cells_x)
    flat = jnp.where(inside_ext, (local_x * cells_y + station_y) * cells_z + station_z, 0)
    values = times_ext.reshape(count, -1)[:, flat]
    arrive_part = jnp.where(owned[None, :], values, 0.0)
    arrivals = lax.psum_scatter(arrive_part, "brick", scatter_dimension=1, tiled=True)
    residual = jnp.where(inside_ext[None, :], values - observed, 0.0)
    source = jnp.zeros((count, extent * cells_y * cells_z), jnp.float32).at[:, flat].add(residual)
    source = source.reshape(count, extent, cells_y, cells_z)
    low_pad = jnp.pad(times_ext, ((0, 0), (1, 1), (1, 1), (1, 1)), constant_values=-big_value)
    weights = [jnp.maximum(other - times_ext, 0.0) / spacing for other in neighbours(low_pad)]
    denom = 1.0 + weights[0] + weights[1] + weights[2] + weights[3] + weights[4] + weights[5]

    def adjoint_group(group, field_own):
        field = extended(field_own, (("brick", 1),), width)
        for inner in range(width):
            padded = jnp.pad(field, ((0, 0), (1, 1), (1, 1), (1, 1)))
            acc = source
            for weight, other in zip(weights, neighbours(padded)):
                acc = acc + weight * other
            field = acc / denom
        return field[:, width : width + cells_x]

    adjoint = lax.fori_loop(
        0, ITERS // width, adjoint_group, jnp.zeros((count, cells_x, cells_y, cells_z), jnp.float32)
    )
    partial_sum = slowness * jnp.sum(adjoint, axis=0)
    kernel = lax.psum_scatter(partial_sum, "src", scatter_dimension=1, tiled=True)
    return (kernel, arrivals)


def solution(mesh):
    in_specs = (P("brick", None, None), P("src"), P("src"), P("src"), P(), P(), P(), P("src", None))
    out_specs = (P("brick", "src", None), P("src", "brick"))
    return jax.shard_map(
        per_device, mesh=mesh, in_specs=in_specs, out_specs=out_specs, check_vma=False
    )
```

profile of v0, /device:TPU:0, one launch (start us, length us, event | category | flops | bytes accessed | tf_op | source)
XLA Modules:
  0.0 400.9 jit_solution(2228122217259365218)
XLA Ops:
  8.1 4.9 %collective-permute-start.4 = (f32[2,64,128]{2,1,0:T(8,128)S(1)}, f32[2,64,128]{2,1,0:T(8,128)S(1)}, u32[]{:S(2)}, u32[]{:S(2)}) collective-permute-start(f32[2,64,128]{2,1,0:T(8,128)S(1)} %get-tuple-element.280), channel_id=1, source_target_pairs={{0,1},{1,2},{2,3},{3,4},{4,5},{5,6},{6,7},{7,8},{8,9},{9,10},{10,1... | collective-permute-start | bytes 196616 | tf_op jit(solution)/shard_map/ppermute | solution.py:22
  20.4 90.8 %while.24 = (s32[]{:T(128)}, f32[2,4,64,128]{3,2,1,0:T(8,128)S(1)}, f32[1,8,64,128]{3,2,1,0:T(8,128)S(1)}, f32[1,8,64,128]{3,2,1,0:T(8,128)S(1)}, f32[1,8,64,128...) while((s32[]{:T(128)}, f32[2,4,64,128]{3,2,1,0:T(8,128)S(1)}, ...), condition=%wide.region_1.2_spmd.clone, body=%wide.region_0.1_spmd.clone.sunk | while | flops 3145762 | bytes 12845277 | solution.py:77
  21.7 4.9 %collective-permute-start.3 = (f32[2,2,64,128]{3,2,1,0:T(8,128)S(1)}, f32[2,2,64,128]{3,2,1,0:T(8,128)S(1)}, u32[]{:S(2)}, u32[]{:S(2)}) collective-permute-start(f32[2,2,64,128]{3,2,1,0:T(8,128)S(1)} %get-tuple-element.425), channel_id=1, source_target_pairs={{0,1},{1,2},{2,3},{3,4},{4,5},{5,6},{6,7},{7,8},{8,9},{9,10},{10,1... | collective-permute-start | bytes 393224 | tf_op jit(solution)/shard_map/while/body/eval_jaxpr/ppermute | solution.py:22
  27.6 3.1 collective-permute-done.3
  33.4 5.0 %collective-permute-start.3 = (f32[2,2,64,128]{3,2,1,0:T(8,128)S(1)}, f32[2,2,64,128]{3,2,1,0:T(8,128)S(1)}, u32[]{:S(2)}, u32[]{:S(2)}) collective-permute-start(f32[2,2,64,128]{3,2,1,0:T(8,128)S(1)} %get-tuple-element.425), channel_id=1, source_target_pairs={{0,1},{1,2},{2,3},{3,4},{4,5},{5,6},{6,7},{7,8},{8,9},{9,10},{10,1... | collective-permute-start | bytes 393224 | tf_op jit(solution)/shard_map/while/body/eval_jaxpr/ppermute | solution.py:22
  39.7 2.6 collective-permute-done.3
  45.0 5.0 %collective-permute-start.3 = (f32[2,2,64,128]{3,2,1,0:T(8,128)S(1)}, f32[2,2,64,128]{3,2,1,0:T(8,128)S(1)}, u32[]{:S(2)}, u32[]{:S(2)}) collective-permute-start(f32[2,2,64,128]{3,2,1,0:T(8,128)S(1)} %get-tuple-element.425), channel_id=1, source_target_pairs={{0,1},{1,2},{2,3},{3,4},{4,5},{5,6},{6,7},{7,8},{8,9},{9,10},{10,1... | collective-permute-start | bytes 393224 | tf_op jit(solution)/shard_map/while/body/eval_jaxpr/ppermute | solution.py:22
  55.2 5.5 %collective-permute-start.3 = (f32[2,2,64,128]{3,2,1,0:T(8,128)S(1)}, f32[2,2,64,128]{3,2,1,0:T(8,128)S(1)}, u32[]{:S(2)}, u32[]{:S(2)}) collective-permute-start(f32[2,2,64,128]{3,2,1,0:T(8,128)S(1)} %get-tuple-element.425), channel_id=1, source_target_pairs={{0,1},{1,2},{2,3},{3,4},{4,5},{5,6},{6,7},{7,8},{8,9},{9,10},{10,1... | collective-permute-start | bytes 393224 | tf_op jit(solution)/shard_map/while/body/eval_jaxpr/ppermute | solution.py:22
  65.9 5.9 %collective-permute-start.3 = (f32[2,2,64,128]{3,2,1,0:T(8,128)S(1)}, f32[2,2,64,128]{3,2,1,0:T(8,128)S(1)}, u32[]{:S(2)}, u32[]{:S(2)}) collective-permute-start(f32[2,2,64,128]{3,2,1,0:T(8,128)S(1)} %get-tuple-element.425), channel_id=1, source_target_pairs={{0,1},{1,2},{2,3},{3,4},{4,5},{5,6},{6,7},{7,8},{8,9},{9,10},{10,1... | collective-permute-start | bytes 393224 | tf_op jit(solution)/shard_map/while/body/eval_jaxpr/ppermute | solution.py:22
  76.9 6.0 %collective-permute-start.3 = (f32[2,2,64,128]{3,2,1,0:T(8,128)S(1)}, f32[2,2,64,128]{3,2,1,0:T(8,128)S(1)}, u32[]{:S(2)}, u32[]{:S(2)}) collective-permute-start(f32[2,2,64,128]{3,2,1,0:T(8,128)S(1)} %get-tuple-element.425), channel_id=1, source_target_pairs={{0,1},{1,2},{2,3},{3,4},{4,5},{5,6},{6,7},{7,8},{8,9},{9,10},{10,1... | collective-permute-start | bytes 393224 | tf_op jit(solution)/shard_map/while/body/eval_jaxpr/ppermute | solution.py:22
  88.1 5.9 %collective-permute-start.3 = (f32[2,2,64,128]{3,2,1,0:T(8,128)S(1)}, f32[2,2,64,128]{3,2,1,0:T(8,128)S(1)}, u32[]{:S(2)}, u32[]{:S(2)}) collective-permute-start(f32[2,2,64,128]{3,2,1,0:T(8,128)S(1)} %get-tuple-element.425), channel_id=1, source_target_pairs={{0,1},{1,2},{2,3},{3,4},{4,5},{5,6},{6,7},{7,8},{8,9},{9,10},{10,1... | collective-permute-start | bytes 393224 | tf_op jit(solution)/shard_map/while/body/eval_jaxpr/ppermute | solution.py:22
  99.3 8.0 %collective-permute-start.3 = (f32[2,2,64,128]{3,2,1,0:T(8,128)S(1)}, f32[2,2,64,128]{3,2,1,0:T(8,128)S(1)}, u32[]{:S(2)}, u32[]{:S(2)}) collective-permute-start(f32[2,2,64,128]{3,2,1,0:T(8,128)S(1)} %get-tuple-element.425), channel_id=1, source_target_pairs={{0,1},{1,2},{2,3},{3,4},{4,5},{5,6},{6,7},{7,8},{8,9},{9,10},{10,1... | collective-permute-start | bytes 393224 | tf_op jit(solution)/shard_map/while/body/eval_jaxpr/ppermute | solution.py:22
  111.2 6.4 %collective-permute-start.6 = (f32[2,2,64,128]{3,2,1,0:T(8,128)S(1)}, f32[2,2,64,128]{3,2,1,0:T(8,128)S(1)}, u32[]{:S(2)}, u32[]{:S(2)}) collective-permute-start(f32[2,2,64,128]{3,2,1,0:T(8,128)S(1)} %get-tuple-element.273), channel_id=1, source_target_pairs={{0,1},{1,2},{2,3},{3,4},{4,5},{5,6},{6,7},{7,8},{8,9},{9,10},{10,1... | collective-permute-start | bytes 393224 | tf_op jit(solution)/shard_map/ppermute | solution.py:22
  119.3 2.1 collective-permute-done.6
  121.5 4.7 %collective-permute-done.7 = f32[2,2,64,128]{3,2,1,0:T(8,128)S(1)} collective-permute-done((f32[2,2,64,128]{3,2,1,0:T(8,128)S(1)}, f32[2,2,64,128]{3,2,1,0:T(8,128)S(1)}, u32[]{:S(2)}, u32[]{:S(2)}) %collective-permute-start.7) | collective-permute-done | bytes 131104 | tf_op jit(solution)/shard_map/ppermute | solution.py:24
  126.2 16.6 %copy.10 = f32[2,8,64,128]{0,3,2,1:T(8,128)} copy(f32[2,8,64,128]{3,2,1,0:T(8,128)S(1)} %constant_dynamic-update-slice_fusion) | data formatting | bytes 1048576 | tf_op jit(solution)/shard_map/concatenate | solution.py:20
  143.8 35.6 %bitcast_select_fusion = f32[2,65536]{0,1:T(8,128)} fusion(f32[2,8,64,128]{0,3,2,1:T(8,128)} %copy.10, pred[65536]{0:T(1024)(128)(4,1)S(1)} %bitcast.52), kind=kLoop, calls=%fused_computation.88 | loop fusion | flops 131072 | bytes 1114112 | tf_op jit(solution)/shard_map/jit(_where)/select_n | solution.py:79
  179.5 16.0 %gather_fusion = f32[2048,2]{1,0:T(8,128)S(1)} fusion(f32[2,65536]{0,1:T(8,128)} %bitcast_select_fusion, s32[2048]{0:T(1024)S(1)} %get-tuple-element.254), kind=kCustom, calls=%fused_computation | custom fusion | bytes 40960 | tf_op jit(solution)/shard_map/gather | solution.py:84
  195.5 28.0 %scatter_custom_fusion = f32[2,65536]{0,1:T(8,128)} fusion(s32[2048]{0:T(1024)S(1)} %get-tuple-element.255, f32[]{:T(128)} %constant.20.clone.1, f32[2,2048]{0,1:T(8,128)S(1)} %copy.11, f32[2048,2]{1,0:T(8,128)S(1)} %gather_fusion, pred[2048]{0:T(1024)(128)(4,1)S(1)} %get-tuple-element.283), kind=kCustom, calls=%fused_computation.89 | custom fusion | flops 12288 | bytes 2624512 | tf_op jit(solution)/shard_map/scatter-add | solution.py:88
  223.5 19.4 %copy.12 = f32[2,8,64,128]{3,2,1,0:T(8,128)S(1)} copy(f32[2,8,64,128]{0,3,2,1:T(8,128)} %bitcast.39) | data formatting | bytes 1048576 | tf_op jit(solution)/shard_map/while | solution.py:104
  242.9 4.2 %add_add_fusion = (f32[2,8,64,128]{3,2,1,0:T(8,128)S(1)}, f32[2,8,64,128]{3,2,1,0:T(8,128)S(1)}, f32[2,8,64,128]{3,2,1,0:T(8,128)S(1)}, f32[2,8,64,128]{3,2,1,0:...) fusion(f32[2,8,64,128]{3,2,1,0:T(8,128)} %broadcast_select_fusion), kind=kLoop, calls=%fused_computation.125 | loop fusion | flops 3145728 | bytes 4194304 | tf_op jit(solution)/shard_map/add | solution.py:92
  248.6 122.1 %while.23 = (s32[]{:T(128)}, f32[2,4,64,128]{3,2,1,0:T(8,128)S(1)}, f32[2,8,64,128]{3,2,1,0:T(8,128)S(1)}, f32[2,8,64,128]{3,2,1,0:T(8,128)S(1)}, f32[2,8,64,128...) while((s32[]{:T(128)}, f32[2,4,64,128]{3,2,1,0:T(8,128)S(1)}, ...), condition=%wide.region_4.5_spmd, body=%wide.region_3.4_spmd.sunk | while | flops 6527714 | bytes 23231028 | solution.py:104
  250.5 6.5 %collective-permute-start.1 = (f32[2,2,64,128]{3,2,1,0:T(8,128)S(1)}, f32[2,2,64,128]{3,2,1,0:T(8,128)}, u32[]{:S(2)}, u32[]{:S(2)}) collective-permute-start(f32[2,2,64,128]{3,2,1,0:T(8,128)S(1)} %get-tuple-element.408), channel_id=1, source_target_pairs={{0,1},{1,2},{2,3},{3,4},{4,5},{5,6},{6,7},{7,8},{8,9},{9,10},{10,1... | collective-permute-start | bytes 393224 | tf_op jit(solution)/shard_map/while/body/eval_jaxpr/ppermute | solution.py:22
  265.0 6.8 %collective-permute-start.1 = (f32[2,2,64,128]{3,2,1,0:T(8,128)S(1)}, f32[2,2,64,128]{3,2,1,0:T(8,128)}, u32[]{:S(2)}, u32[]{:S(2)}) collective-permute-start(f32[2,2,64,128]{3,2,1,0:T(8,128)S(1)} %get-tuple-element.408), channel_id=1, source_target_pairs={{0,1},{1,2},{2,3},{3,4},{4,5},{5,6},{6,7},{7,8},{8,9},{9,10},{10,1... | collective-permute-start | bytes 393224 | tf_op jit(solution)/shard_map/while/body/eval_jaxpr/ppermute | solution.py:22
  280.0 6.7 %collective-permute-start.1 = (f32[2,2,64,128]{3,2,1,0:T(8,128)S(1)}, f32[2,2,64,128]{3,2,1,0:T(8,128)}, u32[]{:S(2)}, u32[]{:S(2)}) collective-permute-start(f32[2,2,64,128]{3,2,1,0:T(8,128)S(1)} %get-tuple-element.408), channel_id=1, source_target_pairs={{0,1},{1,2},{2,3},{3,4},{4,5},{5,6},{6,7},{7,8},{8,9},{9,10},{10,1... | collective-permute-start | bytes 393224 | tf_op jit(solution)/shard_map/while/body/eval_jaxpr/ppermute | solution.py:22
  294.0 9.9 %collective-permute-start.1 = (f32[2,2,64,128]{3,2,1,0:T(8,128)S(1)}, f32[2,2,64,128]{3,2,1,0:T(8,128)}, u32[]{:S(2)}, u32[]{:S(2)}) collective-permute-start(f32[2,2,64,128]{3,2,1,0:T(8,128)S(1)} %get-tuple-element.408), channel_id=1, source_target_pairs={{0,1},{1,2},{2,3},{3,4},{4,5},{5,6},{6,7},{7,8},{8,9},{9,10},{10,1... | collective-permute-start | bytes 393224 | tf_op jit(solution)/shard_map/while/body/eval_jaxpr/ppermute | solution.py:22
  303.9 2.4 collective-permute-done
  311.3 8.3 %collective-permute-start.1 = (f32[2,2,64,128]{3,2,1,0:T(8,128)S(1)}, f32[2,2,64,128]{3,2,1,0:T(8,128)}, u32[]{:S(2)}, u32[]{:S(2)}) collective-permute-start(f32[2,2,64,128]{3,2,1,0:T(8,128)S(1)} %get-tuple-element.408), channel_id=1, source_target_pairs={{0,1},{1,2},{2,3},{3,4},{4,5},{5,6},{6,7},{7,8},{8,9},{9,10},{10,1... | collective-permute-start | bytes 393224 | tf_op jit(solution)/shard_map/while/body/eval_jaxpr/ppermute | solution.py:22
  326.5 7.8 %collective-permute-start.1 = (f32[2,2,64,128]{3,2,1,0:T(8,128)S(1)}, f32[2,2,64,128]{3,2,1,0:T(8,128)}, u32[]{:S(2)}, u32[]{:S(2)}) collective-permute-start(f32[2,2,64,128]{3,2,1,0:T(8,128)S(1)} %get-tuple-element.408), channel_id=1, source_target_pairs={{0,1},{1,2},{2,3},{3,4},{4,5},{5,6},{6,7},{7,8},{8,9},{9,10},{10,1... | collective-permute-start | bytes 393224 | tf_op jit(solution)/shard_map/while/body/eval_jaxpr/ppermute | solution.py:22
  341.1 10.6 %collective-permute-start.1 = (f32[2,2,64,128]{3,2,1,0:T(8,128)S(1)}, f32[2,2,64,128]{3,2,1,0:T(8,128)}, u32[]{:S(2)}, u32[]{:S(2)}) collective-permute-start(f32[2,2,64,128]{3,2,1,0:T(8,128)S(1)} %get-tuple-element.408), channel_id=1, source_target_pairs={{0,1},{1,2},{2,3},{3,4},{4,5},{5,6},{6,7},{7,8},{8,9},{9,10},{10,1... | collective-permute-start | bytes 393224 | tf_op jit(solution)/shard_map/while/body/eval_jaxpr/ppermute | solution.py:22
  358.5 7.2 %collective-permute-start.1 = (f32[2,2,64,128]{3,2,1,0:T(8,128)S(1)}, f32[2,2,64,128]{3,2,1,0:T(8,128)}, u32[]{:S(2)}, u32[]{:S(2)}) collective-permute-start(f32[2,2,64,128]{3,2,1,0:T(8,128)S(1)} %get-tuple-element.408), channel_id=1, source_target_pairs={{0,1},{1,2},{2,3},{3,4},{4,5},{5,6},{6,7},{7,8},{8,9},{9,10},{10,1... | collective-permute-start | bytes 393224 | tf_op jit(solution)/shard_map/while/body/eval_jaxpr/ppermute | solution.py:22
  373.8 20.3 %reduce-scatter.3.cloned.1.call-done = f32[4,32,128]{2,1,0:T(8,128)} async-done(((f32[4,64,128]{2,1,0:T(8,128)}), f32[4,32,128]{2,1,0:T(8,128)}) %reduce-scatter.3.cloned.1.call-update) | async-done | bytes 65552 | tf_op jit(solution)/shard_map/reduce_scatter | solution.py:108
  (249 shorter events, 108.9 us)
Async XLA Ops:
  7.2 365.1 %reduce-scatter.5.cloned.1.call-start = ((), (), s32[]{:S(2)}) async-start(), calls=%async_computation.3 | async-start | bytes 1114112 | tf_op jit(solution)/shard_map/reduce_scatter | solution.py:86
  8.1 9.4 %collective-permute-start.4 = (f32[2,64,128]{2,1,0:T(8,128)S(1)}, f32[2,64,128]{2,1,0:T(8,128)S(1)}, u32[]{:S(2)}, u32[]{:S(2)}) collective-permute-start(f32[2,64,128]{2,1,0:T(8,128)S(1)} %get-tuple-element.280), channel_id=1, source_target_pairs={{0,1},{1,2},{2,3},{3,4},{4,5},{5,6},{6,7},{7,8},{8,9},{9,10},{10,1... | collective-permute-start | bytes 196616 | tf_op jit(solution)/shard_map/ppermute | solution.py:22
  21.7 9.0 %collective-permute-start.3 = (f32[2,2,64,128]{3,2,1,0:T(8,128)S(1)}, f32[2,2,64,128]{3,2,1,0:T(8,128)S(1)}, u32[]{:S(2)}, u32[]{:S(2)}) collective-permute-start(f32[2,2,64,128]{3,2,1,0:T(8,128)S(1)} %get-tuple-element.425), channel_id=1, source_target_pairs={{0,1},{1,2},{2,3},{3,4},{4,5},{5,6},{6,7},{7,8},{8,9},{9,10},{10,1... | collective-permute-start | bytes 393224 | tf_op jit(solution)/shard_map/while/body/eval_jaxpr/ppermute | solution.py:22
  33.4 8.9 %collective-permute-start.3 = (f32[2,2,64,128]{3,2,1,0:T(8,128)S(1)}, f32[2,2,64,128]{3,2,1,0:T(8,128)S(1)}, u32[]{:S(2)}, u32[]{:S(2)}) collective-permute-start(f32[2,2,64,128]{3,2,1,0:T(8,128)S(1)} %get-tuple-element.425), channel_id=1, source_target_pairs={{0,1},{1,2},{2,3},{3,4},{4,5},{5,6},{6,7},{7,8},{8,9},{9,10},{10,1... | collective-permute-start | bytes 393224 | tf_op jit(solution)/shard_map/while/body/eval_jaxpr/ppermute | solution.py:22
  43.7 8.4 %collective-permute-start.2 = (f32[2,2,64,128]{3,2,1,0:T(8,128)S(1)}, f32[2,2,64,128]{3,2,1,0:T(8,128)S(1)}, u32[]{:S(2)}, u32[]{:S(2)}) collective-permute-start(f32[2,2,64,128]{3,2,1,0:T(8,128)S(1)} %get-tuple-element.424), channel_id=1, source_target_pairs={{1,0},{2,1},{3,2},{4,3},{5,4},{6,5},{7,6},{8,7},{9,8},{10,9},{11,1... | collective-permute-start | bytes 393224 | tf_op jit(solution)/shard_map/while/body/eval_jaxpr/ppermute | solution.py:24
  53.9 8.5 %collective-permute-start.2 = (f32[2,2,64,128]{3,2,1,0:T(8,128)S(1)}, f32[2,2,64,128]{3,2,1,0:T(8,128)S(1)}, u32[]{:S(2)}, u32[]{:S(2)}) collective-permute-start(f32[2,2,64,128]{3,2,1,0:T(8,128)S(1)} %get-tuple-element.424), channel_id=1, source_target_pairs={{1,0},{2,1},{3,2},{4,3},{5,4},{6,5},{7,6},{8,7},{9,8},{10,9},{11,1... | collective-permute-start | bytes 393224 | tf_op jit(solution)/shard_map/while/body/eval_jaxpr/ppermute | solution.py:24
  64.6 9.3 %collective-permute-start.2 = (f32[2,2,64,128]{3,2,1,0:T(8,128)S(1)}, f32[2,2,64,128]{3,2,1,0:T(8,128)S(1)}, u32[]{:S(2)}, u32[]{:S(2)}) collective-permute-start(f32[2,2,64,128]{3,2,1,0:T(8,128)S(1)} %get-tuple-element.424), channel_id=1, source_target_pairs={{1,0},{2,1},{3,2},{4,3},{5,4},{6,5},{7,6},{8,7},{9,8},{10,9},{11,1... | collective-permute-start | bytes 393224 | tf_op jit(solution)/shard_map/while/body/eval_jaxpr/ppermute | solution.py:24
  65.9 8.4 %collective-permute-start.3 = (f32[2,2,64,128]{3,2,1,0:T(8,128)S(1)}, f32[2,2,64,128]{3,2,1,0:T(8,128)S(1)}, u32[]{:S(2)}, u32[]{:S(2)}) collective-permute-start(f32[2,2,64,128]{3,2,1,0:T(8,128)S(1)} %get-tuple-element.425), channel_id=1, source_target_pairs={{0,1},{1,2},{2,3},{3,4},{4,5},{5,6},{6,7},{7,8},{8,9},{9,10},{10,1... | collective-permute-start | bytes 393224 | tf_op jit(solution)/shard_map/while/body/eval_jaxpr/ppermute | solution.py:22
  75.6 9.6 %collective-permute-start.2 = (f32[2,2,64,128]{3,2,1,0:T(8,128)S(1)}, f32[2,2,64,128]{3,2,1,0:T(8,128)S(1)}, u32[]{:S(2)}, u32[]{:S(2)}) collective-permute-start(f32[2,2,64,128]{3,2,1,0:T(8,128)S(1)} %get-tuple-element.424), channel_id=1, source_target_pairs={{1,0},{2,1},{3,2},{4,3},{5,4},{6,5},{7,6},{8,7},{9,8},{10,9},{11,1... | collective-permute-start | bytes 393224 | tf_op jit(solution)/shard_map/while/body/eval_jaxpr/ppermute | solution.py:24
  76.9 8.5 %collective-permute-start.3 = (f32[2,2,64,128]{3,2,1,0:T(8,128)S(1)}, f32[2,2,64,128]{3,2,1,0:T(8,128)S(1)}, u32[]{:S(2)}, u32[]{:S(2)}) collective-permute-start(f32[2,2,64,128]{3,2,1,0:T(8,128)S(1)} %get-tuple-element.425), channel_id=1, source_target_pairs={{0,1},{1,2},{2,3},{3,4},{4,5},{5,6},{6,7},{7,8},{8,9},{9,10},{10,1... | collective-permute-start | bytes 393224 | tf_op jit(solution)/shard_map/while/body/eval_jaxpr/ppermute | solution.py:22
  86.8 9.4 %collective-permute-start.2 = (f32[2,2,64,128]{3,2,1,0:T(8,128)S(1)}, f32[2,2,64,128]{3,2,1,0:T(8,128)S(1)}, u32[]{:S(2)}, u32[]{:S(2)}) collective-permute-start(f32[2,2,64,128]{3,2,1,0:T(8,128)S(1)} %get-tuple-element.424), channel_id=1, source_target_pairs={{1,0},{2,1},{3,2},{4,3},{5,4},{6,5},{7,6},{8,7},{9,8},{10,9},{11,1... | collective-permute-start | bytes 393224 | tf_op jit(solution)/shard_map/while/body/eval_jaxpr/ppermute | solution.py:24
  88.1 8.4 %collective-permute-start.3 = (f32[2,2,64,128]{3,2,1,0:T(8,128)S(1)}, f32[2,2,64,128]{3,2,1,0:T(8,128)S(1)}, u32[]{:S(2)}, u32[]{:S(2)}) collective-permute-start(f32[2,2,64,128]{3,2,1,0:T(8,128)S(1)} %get-tuple-element.425), channel_id=1, source_target_pairs={{0,1},{1,2},{2,3},{3,4},{4,5},{5,6},{6,7},{7,8},{8,9},{9,10},{10,1... | collective-permute-start | bytes 393224 | tf_op jit(solution)/shard_map/while/body/eval_jaxpr/ppermute | solution.py:22
  98.0 10.3 %collective-permute-start.2 = (f32[2,2,64,128]{3,2,1,0:T(8,128)S(1)}, f32[2,2,64,128]{3,2,1,0:T(8,128)S(1)}, u32[]{:S(2)}, u32[]{:S(2)}) collective-permute-start(f32[2,2,64,128]{3,2,1,0:T(8,128)S(1)} %get-tuple-element.424), channel_id=1, source_target_pairs={{1,0},{2,1},{3,2},{4,3},{5,4},{6,5},{7,6},{8,7},{9,8},{10,9},{11,1... | collective-permute-start | bytes 393224 | tf_op jit(solution)/shard_map/while/body/eval_jaxpr/ppermute | solution.py:24
  99.3 10.5 %collective-permute-start.3 = (f32[2,2,64,128]{3,2,1,0:T(8,128)S(1)}, f32[2,2,64,128]{3,2,1,0:T(8,128)S(1)}, u32[]{:S(2)}, u32[]{:S(2)}) collective-permute-start(f32[2,2,64,128]{3,2,1,0:T(8,128)S(1)} %get-tuple-element.425), channel_id=1, source_target_pairs={{0,1},{1,2},{2,3},{3,4},{4,5},{5,6},{6,7},{7,8},{8,9},{9,10},{10,1... | collective-permute-start | bytes 393224 | tf_op jit(solution)/shard_map/while/body/eval_jaxpr/ppermute | solution.py:22
  111.2 10.3 %collective-permute-start.6 = (f32[2,2,64,128]{3,2,1,0:T(8,128)S(1)}, f32[2,2,64,128]{3,2,1,0:T(8,128)S(1)}, u32[]{:S(2)}, u32[]{:S(2)}) collective-permute-start(f32[2,2,64,128]{3,2,1,0:T(8,128)S(1)} %get-tuple-element.273), channel_id=1, source_target_pairs={{0,1},{1,2},{2,3},{3,4},{4,5},{5,6},{6,7},{7,8},{8,9},{9,10},{10,1... | collective-permute-start | bytes 393224 | tf_op jit(solution)/shard_map/ppermute | solution.py:22
  248.5 145.5 %reduce-scatter.3.cloned.1.call-start = ((), (), s32[]{:S(2)}) async-start(), calls=%async_computation.2 | async-start | bytes 196608 | tf_op jit(solution)/shard_map/reduce_scatter | solution.py:108
  249.2 9.9 %collective-permute-start = (f32[2,2,64,128]{3,2,1,0:T(8,128)}, f32[2,2,64,128]{3,2,1,0:T(8,128)}, u32[]{:S(2)}, u32[]{:S(2)}) collective-permute-start(f32[2,2,64,128]{3,2,1,0:T(8,128)} %get-tuple-element.407), channel_id=1, source_target_pairs={{1,0},{2,1},{3,2},{4,3},{5,4},{6,5},{7,6},{8,7},{9,8},{10,9},{11,1... | collective-permute-start | bytes 393224 | tf_op jit(solution)/shard_map/while/body/eval_jaxpr/ppermute | solution.py:24
  250.5 9.5 %collective-permute-start.1 = (f32[2,2,64,128]{3,2,1,0:T(8,128)S(1)}, f32[2,2,64,128]{3,2,1,0:T(8,128)}, u32[]{:S(2)}, u32[]{:S(2)}) collective-permute-start(f32[2,2,64,128]{3,2,1,0:T(8,128)S(1)} %get-tuple-element.408), channel_id=1, source_target_pairs={{0,1},{1,2},{2,3},{3,4},{4,5},{5,6},{6,7},{7,8},{8,9},{9,10},{10,1... | collective-permute-start | bytes 393224 | tf_op jit(solution)/shard_map/while/body/eval_jaxpr/ppermute | solution.py:22
  263.7 10.0 %collective-permute-start = (f32[2,2,64,128]{3,2,1,0:T(8,128)}, f32[2,2,64,128]{3,2,1,0:T(8,128)}, u32[]{:S(2)}, u32[]{:S(2)}) collective-permute-start(f32[2,2,64,128]{3,2,1,0:T(8,128)} %get-tuple-element.407), channel_id=1, source_target_pairs={{1,0},{2,1},{3,2},{4,3},{5,4},{6,5},{7,6},{8,7},{9,8},{10,9},{11,1... | collective-permute-start | bytes 393224 | tf_op jit(solution)/shard_map/while/body/eval_jaxpr/ppermute | solution.py:24
  265.0 10.0 %collective-permute-start.1 = (f32[2,2,64,128]{3,2,1,0:T(8,128)S(1)}, f32[2,2,64,128]{3,2,1,0:T(8,128)}, u32[]{:S(2)}, u32[]{:S(2)}) collective-permute-start(f32[2,2,64,128]{3,2,1,0:T(8,128)S(1)} %get-tuple-element.408), channel_id=1, source_target_pairs={{0,1},{1,2},{2,3},{3,4},{4,5},{5,6},{6,7},{7,8},{8,9},{9,10},{10,1... | collective-permute-start | bytes 393224 | tf_op jit(solution)/shard_map/while/body/eval_jaxpr/ppermute | solution.py:22
  278.7 9.0 %collective-permute-start = (f32[2,2,64,128]{3,2,1,0:T(8,128)}, f32[2,2,64,128]{3,2,1,0:T(8,128)}, u32[]{:S(2)}, u32[]{:S(2)}) collective-permute-start(f32[2,2,64,128]{3,2,1,0:T(8,128)} %get-tuple-element.407), channel_id=1, source_target_pairs={{1,0},{2,1},{3,2},{4,3},{5,4},{6,5},{7,6},{8,7},{9,8},{10,9},{11,1... | collective-permute-start | bytes 393224 | tf_op jit(solution)/shard_map/while/body/eval_jaxpr/ppermute | solution.py:24
  280.0 9.0 %collective-permute-start.1 = (f32[2,2,64,128]{3,2,1,0:T(8,128)S(1)}, f32[2,2,64,128]{3,2,1,0:T(8,128)}, u32[]{:S(2)}, u32[]{:S(2)}) collective-permute-start(f32[2,2,64,128]{3,2,1,0:T(8,128)S(1)} %get-tuple-element.408), channel_id=1, source_target_pairs={{0,1},{1,2},{2,3},{3,4},{4,5},{5,6},{6,7},{7,8},{8,9},{9,10},{10,1... | collective-permute-start | bytes 393224 | tf_op jit(solution)/shard_map/while/body/eval_jaxpr/ppermute | solution.py:22
  292.7 13.6 %collective-permute-start = (f32[2,2,64,128]{3,2,1,0:T(8,128)}, f32[2,2,64,128]{3,2,1,0:T(8,128)}, u32[]{:S(2)}, u32[]{:S(2)}) collective-permute-start(f32[2,2,64,128]{3,2,1,0:T(8,128)} %get-tuple-element.407), channel_id=1, source_target_pairs={{1,0},{2,1},{3,2},{4,3},{5,4},{6,5},{7,6},{8,7},{9,8},{10,9},{11,1... | collective-permute-start | bytes 393224 | tf_op jit(solution)/shard_map/while/body/eval_jaxpr/ppermute | solution.py:24
  294.0 12.3 %collective-permute-start.1 = (f32[2,2,64,128]{3,2,1,0:T(8,128)S(1)}, f32[2,2,64,128]{3,2,1,0:T(8,128)}, u32[]{:S(2)}, u32[]{:S(2)}) collective-permute-start(f32[2,2,64,128]{3,2,1,0:T(8,128)S(1)} %get-tuple-element.408), channel_id=1, source_target_pairs={{0,1},{1,2},{2,3},{3,4},{4,5},{5,6},{6,7},{7,8},{8,9},{9,10},{10,1... | collective-permute-start | bytes 393224 | tf_op jit(solution)/shard_map/while/body/eval_jaxpr/ppermute | solution.py:22
  310.0 10.2 %collective-permute-start = (f32[2,2,64,128]{3,2,1,0:T(8,128)}, f32[2,2,64,128]{3,2,1,0:T(8,128)}, u32[]{:S(2)}, u32[]{:S(2)}) collective-permute-start(f32[2,2,64,128]{3,2,1,0:T(8,128)} %get-tuple-element.407), channel_id=1, source_target_pairs={{1,0},{2,1},{3,2},{4,3},{5,4},{6,5},{7,6},{8,7},{9,8},{10,9},{11,1... | collective-permute-start | bytes 393224 | tf_op jit(solution)/shard_map/while/body/eval_jaxpr/ppermute | solution.py:24
  311.3 10.2 %collective-permute-start.1 = (f32[2,2,64,128]{3,2,1,0:T(8,128)S(1)}, f32[2,2,64,128]{3,2,1,0:T(8,128)}, u32[]{:S(2)}, u32[]{:S(2)}) collective-permute-start(f32[2,2,64,128]{3,2,1,0:T(8,128)S(1)} %get-tuple-element.408), channel_id=1, source_target_pairs={{0,1},{1,2},{2,3},{3,4},{4,5},{5,6},{6,7},{7,8},{8,9},{9,10},{10,1... | collective-permute-start | bytes 393224 | tf_op jit(solution)/shard_map/while/body/eval_jaxpr/ppermute | solution.py:22
  325.2 9.8 %collective-permute-start = (f32[2,2,64,128]{3,2,1,0:T(8,128)}, f32[2,2,64,128]{3,2,1,0:T(8,128)}, u32[]{:S(2)}, u32[]{:S(2)}) collective-permute-start(f32[2,2,64,128]{3,2,1,0:T(8,128)} %get-tuple-element.407), channel_id=1, source_target_pairs={{1,0},{2,1},{3,2},{4,3},{5,4},{6,5},{7,6},{8,7},{9,8},{10,9},{11,1... | collective-permute-start | bytes 393224 | tf_op jit(solution)/shard_map/while/body/eval_jaxpr/ppermute | solution.py:24
  326.5 9.6 %collective-permute-start.1 = (f32[2,2,64,128]{3,2,1,0:T(8,128)S(1)}, f32[2,2,64,128]{3,2,1,0:T(8,128)}, u32[]{:S(2)}, u32[]{:S(2)}) collective-permute-start(f32[2,2,64,128]{3,2,1,0:T(8,128)S(1)} %get-tuple-element.408), channel_id=1, source_target_pairs={{0,1},{1,2},{2,3},{3,4},{4,5},{5,6},{6,7},{7,8},{8,9},{9,10},{10,1... | collective-permute-start | bytes 393224 | tf_op jit(solution)/shard_map/while/body/eval_jaxpr/ppermute | solution.py:22
  339.9 12.5 %collective-permute-start = (f32[2,2,64,128]{3,2,1,0:T(8,128)}, f32[2,2,64,128]{3,2,1,0:T(8,128)}, u32[]{:S(2)}, u32[]{:S(2)}) collective-permute-start(f32[2,2,64,128]{3,2,1,0:T(8,128)} %get-tuple-element.407), channel_id=1, source_target_pairs={{1,0},{2,1},{3,2},{4,3},{5,4},{6,5},{7,6},{8,7},{9,8},{10,9},{11,1... | collective-permute-start | bytes 393224 | tf_op jit(solution)/shard_map/while/body/eval_jaxpr/ppermute | solution.py:24
  341.1 12.4 %collective-permute-start.1 = (f32[2,2,64,128]{3,2,1,0:T(8,128)S(1)}, f32[2,2,64,128]{3,2,1,0:T(8,128)}, u32[]{:S(2)}, u32[]{:S(2)}) collective-permute-start(f32[2,2,64,128]{3,2,1,0:T(8,128)S(1)} %get-tuple-element.408), channel_id=1, source_target_pairs={{0,1},{1,2},{2,3},{3,4},{4,5},{5,6},{6,7},{7,8},{8,9},{9,10},{10,1... | collective-permute-start | bytes 393224 | tf_op jit(solution)/shard_map/while/body/eval_jaxpr/ppermute | solution.py:22
  357.2 9.2 %collective-permute-start = (f32[2,2,64,128]{3,2,1,0:T(8,128)}, f32[2,2,64,128]{3,2,1,0:T(8,128)}, u32[]{:S(2)}, u32[]{:S(2)}) collective-permute-start(f32[2,2,64,128]{3,2,1,0:T(8,128)} %get-tuple-element.407), channel_id=1, source_target_pairs={{1,0},{2,1},{3,2},{4,3},{5,4},{6,5},{7,6},{8,7},{9,8},{10,9},{11,1... | collective-permute-start | bytes 393224 | tf_op jit(solution)/shard_map/while/body/eval_jaxpr/ppermute | solution.py:24
  358.5 9.1 %collective-permute-start.1 = (f32[2,2,64,128]{3,2,1,0:T(8,128)S(1)}, f32[2,2,64,128]{3,2,1,0:T(8,128)}, u32[]{:S(2)}, u32[]{:S(2)}) collective-permute-start(f32[2,2,64,128]{3,2,1,0:T(8,128)S(1)} %get-tuple-element.408), channel_id=1, source_target_pairs={{0,1},{1,2},{2,3},{3,4},{4,5},{5,6},{6,7},{7,8},{8,9},{9,10},{10,1... | collective-permute-start | bytes 393224 | tf_op jit(solution)/shard_map/while/body/eval_jaxpr/ppermute | solution.py:22
  (26 other events, 330.0 us)
Sparse Core Ops, SparseCore 0:
  248.6 88.2 reduce-scatter.4
  372.4 21.6 reduce-scatter.2
where the time goes:
time: 403 us; the launch traced here: 401 us
  starting transfers between devices  145 us (36%)
  other arithmetic  110 us (27%)
  waiting for transfers between devices  68.9 us (17%)
  local copies, waits for them, and re-layouts  61.4 us (15%)
  between operations  14.3 us (4%)
    ppermute x18, starting transfers between devices, extended(): lax.ppermute(tail, axis, [(i, (i + 1) % count) for i in range(ends)])  121 us
    select_n x2, other arithmetic, per_device(): times_ext = jnp.where(outside, -big_value, times_ext)  36.5 us
    ppermute x18, waiting for transfers between devices, extended(): lax.ppermute(head, axis, [((i + 1) % count, i) for i in range(ends)])  28.9 us
    scatter-add x1, other arithmetic, per_device(): jnp.zeros((count, extent * cells_y * cells_z), jnp.float32).at[:, flat]  28 us
    ppermute x18, starting transfers between devices, extended(): lax.ppermute(head, axis, [((i + 1) % count, i) for i in range(ends)])  23.2 us
    reduce_scatter x1, waiting for transfers between devices, per_device(): lax.psum_scatter(partial_sum, 'src', scatter_dimension=1, tiled=True)  20.3 us
    ppermute x18, waiting for transfers between devices, extended(): lax.ppermute(tail, axis, [(i, (i + 1) % count) for i in range(ends)])  19.7 us
    while x1, local copies, waits for them, and re-layouts, per_device(): lax.fori_loop(0, ITERS // width, adjoint_group, jnp.zeros((count, cells_x...  19.4 us
  transfers between devices with their start and end apart: 38, of which 35 were waited for; matrix products, arithmetic and copies ran while one was open for 9% of the time, Pallas kernels for 0%

commit v1 on v0

v1 whole, which is shorter than its diff:
```python
import functools

import jax
import jax.numpy as jnp
from jax import lax
from jax.experimental import pallas as pl
from jax.experimental.pallas import tpu as pltpu
from jax.sharding import PartitionSpec as P

ITERS = 16

spacing = 0.015625
big_value = 1000000.0
start_slowness = 2.0
half_step = 0.5 * spacing
LOW = 4

VMEM = pl.BlockSpec(memory_space=pltpu.VMEM)
SMEM = pl.BlockSpec(memory_space=pltpu.SMEM)
MESH = pl.DeviceIdType.MESH


def remote(src, dst, send_sem, recv_sem, core, brick):
    return pltpu.make_async_remote_copy(
        src_ref=src,
        dst_ref=dst,
        send_sem=send_sem,
        recv_sem=recv_sem,
        device_id={"src": core, "brick": brick},
        device_id_type=MESH,
    )


def gather_kernel(bricks, slow_ref, full_ref, send_sem, recv_sem, twin_sem, own_sem):
    depth = slow_ref.shape[0]
    half = depth // 2
    lines = bricks // LOW
    me = lax.axis_index("brick")
    core = lax.axis_index("src")
    h = lax.rem(core, 2)
    twin = core + 1 - 2 * h
    line = me // LOW
    bit_x = lax.rem(me, 2)
    bit_y = lax.rem(me // 2, 2)
    flip_x = 1 - 2 * bit_x
    flip_y = 2 - 4 * bit_y
    first = me + flip_x * (1 - h) + flip_y * h
    second = me + flip_y * (1 - h) + flip_x * h
    corner = me + flip_x + flip_y
    has_down = line > 0
    has_up = line < lines - 1

    def piece(q, part):
        return full_ref.at[pl.ds(q * depth + part * half, half)]

    def copy(kind, q, brick, own=False):
        src = slow_ref.at[pl.ds(h * half, half)] if own else piece(q, h)
        return remote(src, piece(q, h), send_sem.at[kind, q], recv_sem.at[q], core, brick)

    def twin_copy(q):
        return remote(piece(q, h), piece(q, h), send_sem.at[4, q], twin_sem.at[q], twin, me)

    barrier = pltpu.get_barrier_semaphore()

    def greet(c, b):
        pl.semaphore_signal(barrier, inc=1, device_id={"src": c, "brick": b}, device_id_type=MESH)

    greet(twin, me)
    greet(core, first)
    greet(core, second)
    pl.when(has_down)(lambda: greet(core, me - LOW))
    pl.when(has_up)(lambda: greet(core, me + LOW))
    pl.semaphore_wait(barrier, 3 + has_down.astype(jnp.int32) + has_up.astype(jnp.int32))

    def sends(q, own, to_down, to_up, wait):
        def go(c):
            c.wait_send() if wait else c.start()

        if to_down is not None:
            pl.when(to_down)(lambda: go(copy(0, q, me - LOW, own)))
        if to_up is not None:
            pl.when(to_up)(lambda: go(copy(1, q, me + LOW, own)))
        go(copy(2, q, first, own))
        go(copy(3, q, second, own))

    own_copy = pltpu.make_async_copy(slow_ref, full_ref.at[pl.ds(me * depth, depth)], own_sem)
    sends(me, True, has_down, has_up, False)
    own_copy.start()

    def arrived(q):
        remote(piece(q, h), piece(q, h), send_sem.at[0, q], recv_sem.at[q], core, first).wait_recv()

    def on_line(base, i, act):
        pl.when((i < lines) & (line >= i))(lambda: act(base - LOW * i, -1))
        pl.when((i < lines) & (line + i < lines))(lambda: act(base + LOW * i, 1))

    def both(base, i, act):
        pl.when(i == 0)(lambda: act(base, 0))
        pl.when(i > 0)(lambda: on_line(base, i, act))

    def from_line(wait):
        def act(q, side):
            if not wait:
                arrived(q)
            sends(q, False, has_down if side > 0 else None, has_up if side < 0 else None, wait)
            c = twin_copy(q)
            c.wait_send() if wait else c.start()

        return act

    def from_first(wait):
        def act(q, side):
            if not wait:
                arrived(q)
            c = copy(3, q, second)
            c.wait_send() if wait else c.start()
            c = twin_copy(q)
            c.wait_send() if wait else c.start()

        return act

    def from_second(wait):
        def act(q, side):
            if not wait:
                arrived(q)
            c = twin_copy(q)
            c.wait_send() if wait else c.start()

        return act

    def turn(i, wait):
        on_line(me, i, from_line(wait))
        both(first, i - 1, from_first(wait))
        both(second, i - 1, from_second(wait))
        pl.when(i >= 2)(lambda: both(corner, i - 2, from_second(wait)))

    @pl.loop(1, lines + 2)
    def _(i):
        turn(i, False)

    own_copy.wait()
    sends(me, True, has_down, has_up, True)

    @pl.loop(1, lines + 2)
    def _(i):
        turn(i, True)

    @pl.loop(0, bricks)
    def _(q):
        @pl.when(q != me)
        def _():
            remote(piece(q, 1 - h), piece(q, 1 - h), send_sem.at[4, q], twin_sem.at[q], twin, me).wait_recv()


def window(pair_depth, grid_x, margin):
    length = min(grid_x, pair_depth + 2 * margin)
    pair = lax.axis_index("brick") // 2
    return jnp.clip(pair * pair_depth - margin, 0, grid_x - length), length


def stations_kernel(grid_x, cells_y, pair_depth, stx_ref, sty_ref, stz_ref, obs_ref, cnt_ref, sum_ref, table):
    rec = stx_ref.shape[1]
    cells_z = cnt_ref.shape[2]
    rows_y = cells_y // 8
    shift = rows_y.bit_length() - 1
    low, length = window(pair_depth, grid_x, ITERS)
    parity = lax.rem(lax.axis_index("brick"), 2)
    sty = sty_ref[...]
    row = (stx_ref[...] - low) * cells_y + (sty & (rows_y - 1)) * 8 + (sty >> shift)
    seen = obs_ref[pl.ds(parity, 1), :]
    hi = seen.astype(jnp.bfloat16).astype(jnp.float32)
    rest = seen - hi
    mid = rest.astype(jnp.bfloat16).astype(jnp.float32)
    lo = rest - mid
    hit = lax.broadcasted_iota(jnp.int32, (cells_z, rec), 0) == stz_ref[...]
    for part, value in enumerate((jnp.ones_like(seen), hi, mid, lo)):
        table[pl.ds(part * cells_z, cells_z), :] = jnp.where(hit, value, 0.0).astype(jnp.bfloat16)
    block = 256
    tiles = block // 8

    @pl.loop(0, length * cells_y // block)
    def _(step):
        rows = lax.broadcasted_iota(jnp.int32, (block, rec), 0) + step * block
        pick = jnp.where(rows == row, 1.0, 0.0).astype(jnp.bfloat16)
        got = lax.dot_general(
            pick, table[...], (((1,), (1,)), ((), ())), preferred_element_type=jnp.float32
        )
        cnt_ref[pl.ds(step * tiles, tiles)] = got[:, :cells_z].reshape(tiles, 8, cells_z)
        total = got[:, cells_z : 2 * cells_z] + (
            got[:, 2 * cells_z : 3 * cells_z] + got[:, 3 * cells_z :]
        )
        sum_ref[pl.ds(step * tiles, tiles)] = total.reshape(tiles, 8, cells_z)


def solve_kernel(
    pair_depth,
    sx_ref,
    sy_ref,
    sz_ref,
    stx_ref,
    sty_ref,
    stz_ref,
    slow_ref,
    cnt_ref,
    sum_ref,
    adj_ref,
    arr_ref,
    time,
    cost,
    picked,
    weight,
    supply,
    field,
):
    grid_x, cells_y, cells_z = slow_ref.shape
    rows = cells_y // 8
    shift = rows.bit_length() - 1
    brick = lax.axis_index("brick")
    parity = lax.rem(brick, 2)
    pair = brick // 2
    lane = lax.broadcasted_iota(jnp.int32, (8, cells_z), 1)
    sub = lax.broadcasted_iota(jnp.int32, (8, cells_z), 0)
    lane_first = lane == 0
    lane_last = lane == cells_z - 1
    sub_first = sub == 0
    sub_last = sub == 7

    def layer_of(ref, x):
        return tuple(ref[x * rows + v] for v in range(rows))

    def y_up(cur, v):
        return cur[v + 1] if v + 1 < rows else pltpu.roll(cur[0], 7, 0)

    def y_down(cur, v):
        return cur[v - 1] if v else pltpu.roll(cur[rows - 1], 1, 0)

    def z_up(one):
        return pltpu.roll(one, cells_z - 1, 1)

    def z_down(one):
        return pltpu.roll(one, 1, 1)

    sx = sx_ref[parity]
    sy = sy_ref[parity]
    sz = sz_ref[parity]
    dz = (lane - sz).astype(jnp.float32)
    flat = []
    for v in range(rows):
        dy = (sub * rows + v - sy).astype(jnp.float32)
        flat.append(dy * dy + dz * dz)

    @pl.loop(0, grid_x)
    def _(x):
        dx = (x - sx).astype(jnp.float32)
        for v in range(rows):
            slow = slow_ref[x, pl.ds(v, 8, stride=rows), :]
            start = (start_slowness * spacing) * jnp.sqrt(dx * dx + flat[v])
            cost[x * rows + v] = (2.0 * half_step) * slow
            time[(x + 1) * rows + v] = start + half_step * slow

    def pads(value):
        for v in range(rows):
            time[v] = jnp.full((8, cells_z), value, jnp.float32)
            time[(grid_x + 1) * rows + v] = jnp.full((8, cells_z), value, jnp.float32)

    pads(big_value)
    group = 2

    def forward(x, prev, cur):
        nxt = layer_of(time, x + 2)
        for v in range(rows):
            one = cur[v]
            up = y_up(cur, v)
            down = y_down(cur, v)
            if v + 1 == rows:
                up = jnp.where(sub_last, big_value, up)
            if v == 0:
                down = jnp.where(sub_first, big_value, down)
            ahead = jnp.where(lane_last, big_value, z_up(one))
            behind = jnp.where(lane_first, big_value, z_down(one))
            low = jnp.minimum(
                jnp.minimum(jnp.minimum(prev[v], nxt[v]), jnp.minimum(up, down)), jnp.minimum(ahead, behind)
            )
            time[(x + 1) * rows + v] = jnp.minimum(one, low + cost[x * rows + v])
        return nxt

    @pl.loop(0, ITERS)
    def _(sweep):
        def body(i, carry):
            prev, cur = carry
            for j in range(group):
                nxt = forward(i * group + j, prev, cur)
                prev, cur = cur, nxt
            return prev, cur

        lax.fori_loop(0, grid_x // group, body, (layer_of(time, 0), layer_of(time, 1)))

    @pl.loop(0, grid_x)
    def _(x):
        for v in range(rows):
            time[(x + 1) * rows + v] = time[(x + 1) * rows + v] - 0.5 * cost[x * rows + v]

    pads(-big_value)

    count = picked.shape[0]
    line = lax.broadcasted_iota(jnp.int32, (1, cells_z), 1)
    unroll = 8

    @pl.loop(0, count // unroll)
    def _(i):
        for j in range(unroll):
            r = pair * count + i * unroll + j
            y = sty_ref[r]
            at = (stx_ref[r] + 1) * rows + (y & (rows - 1))
            got = time[at, pl.ds(y >> shift, 1), :]
            picked[pl.ds(i * unroll + j, 1), :] = jnp.where(line == stz_ref[r], got, 0.0)

    arrived = jnp.sum(jnp.transpose(picked[...]), axis=0, keepdims=True)
    arr_ref[0] = arrived[:, : count // 2]
    arr_ref[1] = arrived[:, count // 2 :]

    base, length = window(pair_depth, grid_x, ITERS - 1)
    outer, _ = window(pair_depth, grid_x, ITERS)

    def weigh(x, prev, cur):
        nxt = layer_of(time, x + 2)
        spot = (x - base) * rows
        for v in range(rows):
            one = cur[v]

            def gain(other):
                return jnp.maximum(other - one, 0.0)

            up = gain(y_up(cur, v))
            down = gain(y_down(cur, v))
            if v + 1 == rows:
                up = jnp.where(sub_last, 0.0, up)
            if v == 0:
                down = jnp.where(sub_first, 0.0, down)
            parts = (
                gain(prev[v]),
                gain(nxt[v]),
                down,
                up,
                jnp.where(lane_first, 0.0, gain(z_down(one))),
                jnp.where(lane_last, 0.0, gain(z_up(one))),
            )
            total = ((parts[0] + parts[1]) + (parts[2] + parts[3])) + (parts[4] + parts[5])
            inverse = 1.0 / (1.0 + total * (1.0 / spacing))
            scaled = inverse * (1.0 / spacing)
            for k, part in enumerate(parts):
                weight[k, spot + v] = part * scaled
            here = (x - outer) * rows + v
            value = (cnt_ref[here] * one - sum_ref[here]) * inverse
            supply[spot + v] = value
            field[spot + rows + v] = value
        return nxt

    def weigh_body(i, carry):
        prev, cur = carry
        for j in range(group):
            nxt = weigh(base + i * group + j, prev, cur)
            prev, cur = cur, nxt
        return prev, cur

    lax.fori_loop(0, length // group, weigh_body, (layer_of(time, base), layer_of(time, base + 1)))
    for v in range(rows):
        field[v] = jnp.zeros((8, cells_z), jnp.float32)
        field[(length + 1) * rows + v] = jnp.zeros((8, cells_z), jnp.float32)

    def backward(x, prev, cur):
        nxt = layer_of(field, x + 2)
        for v in range(rows):
            one = cur[v]
            spot = x * rows + v
            acc = supply[spot] + weight[0, spot] * prev[v]
            acc = acc + weight[1, spot] * nxt[v]
            side = weight[2, spot] * y_down(cur, v) + weight[3, spot] * y_up(cur, v)
            acc = acc + side
            acc = acc + (weight[4, spot] * z_down(one) + weight[5, spot] * z_up(one))
            field[spot + rows] = acc
        return nxt

    @pl.loop(2, ITERS + 1)
    def _(sweep):
        margin = ITERS - sweep
        span = jnp.minimum(grid_x, pair_depth + 2 * margin)
        first = jnp.clip(pair * pair_depth - margin, 0, grid_x - span) - base

        def body(i, carry):
            prev, cur = carry
            for j in range(group):
                nxt = backward(first + i * group + j, prev, cur)
                prev, cur = cur, nxt
            return prev, cur

        lax.fori_loop(0, span // group, body, (layer_of(field, first), layer_of(field, first + 1)))

    mine = pair * pair_depth - base + 1
    for x in range(pair_depth):
        for v in range(rows):
            adj_ref[x, pl.ds(v, 8, stride=rows), :] = field[(mine + x) * rows + v]


def reduce_kernel(cores, adj_ref, arr_ref, out_ref, got_ref, slots, send_sem, recv_sem, word_send, word_recv):
    depth, keep, _ = out_ref.shape
    brick = lax.axis_index("brick")
    core = lax.axis_index("src")
    parity = lax.rem(brick, 2)
    other = brick + 1 - 2 * parity
    me = core * 2 + parity

    def target(k):
        c = lax.rem(core + k // 2, cores)
        p = lax.rem(parity + k % 2, 2)
        return c, p, brick - parity + p

    def copy(k):
        c, p, b = target(k)
        return remote(
            adj_ref.at[pl.ds(p * depth, depth), pl.ds(c * keep, keep)],
            slots.at[k],
            send_sem.at[k],
            recv_sem.at[k],
            c,
            b,
        )

    barrier = pltpu.get_barrier_semaphore()
    for k in range(1, 2 * cores):
        c, _, b = target(k)
        pl.semaphore_signal(barrier, inc=1, device_id={"src": c, "brick": b}, device_id_type=MESH)
    pl.semaphore_wait(barrier, 2 * cores - 1)
    word = remote(arr_ref.at[1 - parity], got_ref.at[parity], word_send, word_recv, core, other)
    word.start()
    for k in range(1, 2 * cores):
        copy(k).start()
    got_ref[parity] = arr_ref[parity]
    total = adj_ref[pl.ds(parity * depth, depth), pl.ds(pl.multiple_of(core * keep, 8), keep), :]
    for k in range(1, 2 * cores):
        copy(k).wait_recv()
        total = total + slots[k]
    out_ref[...] = total
    for k in range(1, 2 * cores):
        copy(k).wait_send()
    word.wait_send()
    remote(arr_ref.at[parity], got_ref.at[1 - parity], word_send, word_recv, core, other).wait_recv()


def per_device(slowness, source_x, source_y, source_z, station_x, station_y, station_z, observed):
    bricks = lax.axis_size("brick")
    cores = lax.axis_size("src")
    depth, cells_y, cells_z = slowness.shape
    grid_x = depth * bricks
    rec = station_x.shape[0]
    pair_depth = 2 * depth
    rows = cells_y // 8
    assert source_x.shape[0] == 2 and bricks % LOW == 0 and cores % 2 == 0
    f32 = jnp.float32

    full = pl.pallas_call(
        functools.partial(gather_kernel, bricks),
        name="gather",
        out_shape=jax.ShapeDtypeStruct((grid_x, cells_y, cells_z), f32),
        in_specs=[VMEM],
        out_specs=VMEM,
        scratch_shapes=[
            pltpu.SemaphoreType.DMA((5, bricks)),
            pltpu.SemaphoreType.DMA((bricks,)),
            pltpu.SemaphoreType.DMA((bricks,)),
            pltpu.SemaphoreType.DMA,
        ],
        compiler_params=pltpu.CompilerParams(collective_id=0, has_side_effects=True),
    )(slowness)

    wide = min(grid_x, pair_depth + 2 * ITERS)
    field = jax.ShapeDtypeStruct((wide * rows, 8, cells_z), f32)
    cnt, total = pl.pallas_call(
        functools.partial(stations_kernel, grid_x, cells_y, pair_depth),
        name="stations",
        out_shape=(field, field),
        in_specs=[VMEM] * 4,
        out_specs=(VMEM, VMEM),
        scratch_shapes=[pltpu.VMEM((4 * cells_z, rec), jnp.bfloat16)],
    )(station_x[None], station_y[None], station_z[None], observed)

    length = min(grid_x, pair_depth + 2 * (ITERS - 1))
    share = rec // bricks
    adj, arr = pl.pallas_call(
        functools.partial(solve_kernel, pair_depth),
        name="solve",
        out_shape=(
            jax.ShapeDtypeStruct((pair_depth, cells_y, cells_z), f32),
            jax.ShapeDtypeStruct((2, 1, share), f32),
        ),
        in_specs=[SMEM] * 6 + [VMEM] * 3,
        out_specs=(VMEM, VMEM),
        scratch_shapes=[
            pltpu.VMEM(((grid_x + 2) * rows, 8, cells_z), f32),
            pltpu.VMEM((grid_x * rows, 8, cells_z), f32),
            pltpu.VMEM((2 * share, cells_z), f32),
            pltpu.VMEM((6, length * rows, 8, cells_z), f32),
            pltpu.VMEM((length * rows, 8, cells_z), f32),
            pltpu.VMEM(((length + 2) * rows, 8, cells_z), f32),
        ],
    )(source_x, source_y, source_z, station_x, station_y, station_z, full, cnt, total)

    keep = cells_y // cores
    summed, arrivals = pl.pallas_call(
        functools.partial(reduce_kernel, cores),
        name="reduce",
        out_shape=(
            jax.ShapeDtypeStruct((depth, keep, cells_z), f32),
            jax.ShapeDtypeStruct((2, 1, share), f32),
        ),
        in_specs=[VMEM, VMEM],
        out_specs=(VMEM, VMEM),
        scratch_shapes=[
            pltpu.VMEM((2 * cores, depth, keep, cells_z), f32),
            pltpu.SemaphoreType.DMA((2 * cores,)),
            pltpu.SemaphoreType.DMA((2 * cores,)),
            pltpu.SemaphoreType.DMA,
            pltpu.SemaphoreType.DMA,
        ],
        compiler_params=pltpu.CompilerParams(collective_id=1, has_side_effects=True),
    )(adj, arr)
    own = lax.dynamic_slice_in_dim(slowness, lax.axis_index("src") * keep, keep, axis=1)
    return own * summed, arrivals[:, 0]


def solution(mesh):
    in_specs = (P("brick", None, None), P("src"), P("src"), P("src"), P(), P(), P(), P("src", None))
    out_specs = (P("brick", "src", None), P("src", "brick"))
    return jax.shard_map(
        per_device, mesh=mesh, in_specs=in_specs, out_specs=out_specs, check_vma=False
    )
```

time: 403 us -> 126 us (0.31)
  starting transfers between devices: 145 us -> 0 us
  Pallas kernels: 0 us -> 122 us
  other arithmetic: 110 us -> 1.48 us
  waiting for transfers between devices: 68.9 us -> 0 us
  local copies, waits for them, and re-layouts: 61.4 us -> 1.23 us
  between operations: 14.3 us -> 0.67 us
    ppermute x36 -> x0, starting transfers between devices: 144 us -> none  [the longest x18 121 us: extended(): lax.ppermute(tail, axis, [(i, (i + 1) % count) for i in range(ends)])]
    pallas_call x0 -> x4, Pallas kernels: none -> 122 us  [the longest x1 79.2 us: per_device(): pl.pallas_call(functools.partial(solve_kernel, pair_depth), name='solve',...]
    ppermute x36 -> x0, waiting for transfers between devices: 48.6 us -> none  [the longest x18 28.9 us: extended(): lax.ppermute(head, axis, [((i + 1) % count, i) for i in range(ends)])]
    select_n x27 -> x0, other arithmetic: 44.3 us -> none  [the longest x2 36.5 us: per_device(): times_ext = jnp.where(outside, -big_value, times_ext)]
    scatter-add x1 -> x0, other arithmetic: 28 us -> none  [per_device(): jnp.zeros((count, extent * cells_y * cells_z), jnp.float32).at[:, flat]]
    reduce_scatter x2 -> x0, waiting for transfers between devices: 20.3 us -> none  [the longest x1 20.3 us: per_device(): lax.psum_scatter(partial_sum, 'src', scatter_dimension=1, tiled=True)]
    while x33 -> x0, local copies, waits for them, and re-layouts: 19.5 us -> none  [the longest x1 19.4 us: per_device(): lax.fori_loop(0, ITERS // width, adjoint_group, jnp.zeros((count, cells_x...]
    concatenate x2 -> x0, local copies, waits for them, and re-layouts: 16.6 us -> none  [extended(): jnp.concatenate([lax.ppermute(tail, axis, [(i, (i + 1) % count) for i in...]
  transfers between devices with their start and end apart: 38 -> 0, of which waited for: 35 -> 0; matrix products, arithmetic and copies ran while one was open for 9% -> 0% of each run, Pallas kernels for 0% -> 0%
where the time goes in v1:
time: 126 us; the launch traced here: 125 us
  Pallas kernels  122 us (97%)
  other arithmetic  1.48 us (1%)
    pallas_call x1, Pallas kernels, per_device(): pl.pallas_call(functools.partial(solve_kernel, pair_depth), name='solve',...  79.2 us
    pallas_call x1, Pallas kernels, per_device(): pl.pallas_call(functools.partial(gather_kernel, bricks), name='gather', o...  25.2 us
    pallas_call x1, Pallas kernels, per_device(): pl.pallas_call(functools.partial(stations_kernel, grid_x, cells_y, pair_d...  10.1 us
    pallas_call x1, Pallas kernels, per_device(): pl.pallas_call(functools.partial(reduce_kernel, cores), name='reduce', ou...  7.37 us

profile of v1, /device:TPU:0, one launch (start us, length us, event | category | flops | bytes accessed | tf_op | source)
XLA Modules:
  0.0 125.3 jit_solution(9880726879936671475)
XLA Ops:
  0.6 10.1 %stations.1 = (f32[320,8,128]{2,1,0:T(8,128)}, f32[320,8,128]{2,1,0:T(8,128)}) custom-call(s32[1,2048]{1,0:T(1,128)} %bitcast.4, s32[1,2048]{1,0:T(1,128)} %bitcast.5, s32[1,2048]{1,0:T(1,128)} %bitcast.6, f32[2,2048]{1,0:T(2,128)} %obs_ref.1), custom_call_target="tpu_custom_call" | custom-call | tf_op jit(solution)/shard_map/stations/pallas_call | solution.py:478
  10.8 25.2 %gather.1.slow_ref = f32[64,64,128]{2,1,0:T(8,128)} custom-call(f32[4,64,128]{2,1,0:T(8,128)} %slow_ref.1), custom_call_target="tpu_custom_call" | custom-call | tf_op jit(solution)/shard_map/gather/pallas_call | solution.py:461
  35.9 0.0 copy-start
  36.0 79.2 %solve.1 = (f32[8,64,128]{2,1,0:T(8,128)}, f32[2,1,128]{2,1,0:T(1,128)}) custom-call(s32[2]{0:T(128)} %sx_ref.1, s32[2]{0:T(128)} %sy_ref.1, s32[2]{0:T(128)} %sz_ref.1, s32[2048]{0:T(1024)} %stx_ref.1, s32[2048]{0:T(1024)} %sty_ref.1, s32[2048]{0:T(1024)} %stz_ref.1, f32[64,64,128]{2,1,0:T(8,128)} %gather.1.slow_ref, ...), custom_call_target="tpu_custom_call" | custom-call | tf_op jit(solution)/shard_map/solve/pallas_call | solution.py:489
  115.2 7.4 %reduce.1 = (f32[4,32,128]{2,1,0:T(8,128)}, f32[2,1,128]{2,1,0:T(1,128)}) custom-call(f32[8,64,128]{2,1,0:T(8,128)} %get-tuple-element.10.adj_ref, f32[2,1,128]{2,1,0:T(1,128)} %get-tuple-element.11.arr_ref), custom_call_target="tpu_custom_call" | custom-call | tf_op jit(solution)/shard_map/reduce/pallas_call | solution.py:509
  122.6 0.0 copy-done
  122.6 1.5 %dynamic-slice_multiply_fusion = f32[4,32,128]{2,1,0:T(8,128)} fusion(f32[4,32,128]{2,1,0:T(8,128)} %get-tuple-element.12, f32[4,64,128]{2,1,0:T(8,128)S(1)} %copy-done, s32[]{:T(128)S(6)} %select_n.3), kind=kLoop, calls=%fused_computation | loop fusion | flops 16384 | bytes 196612 | tf_op jit(solution)/shard_map/mul | solution.py:528
  124.1 1.2 copy.11
Async XLA Ops:
  35.9 86.6 %copy-start = (f32[4,64,128]{2,1,0:T(8,128)S(1)}, f32[4,64,128]{2,1,0:T(8,128)}, u32[]{:S(2)}) copy-start(f32[4,64,128]{2,1,0:T(8,128)} %slow_ref.1) | copy-start | bytes 393220

commit v2 on v1

--- a/solution.py
+++ b/solution.py
@@ -14,6 +14,8 @@
 start_slowness = 2.0
 half_step = 0.5 * spacing
 LOW = 4
+FORWARD = 8
+BACKWARD = 4
 
 VMEM = pl.BlockSpec(memory_space=pltpu.VMEM)
 SMEM = pl.BlockSpec(memory_space=pltpu.SMEM)
@@ -31,134 +33,13 @@
     )
 
 
-def gather_kernel(bricks, slow_ref, full_ref, send_sem, recv_sem, twin_sem, own_sem):
-    depth = slow_ref.shape[0]
-    half = depth // 2
-    lines = bricks // LOW
-    me = lax.axis_index("brick")
-    core = lax.axis_index("src")
-    h = lax.rem(core, 2)
-    twin = core + 1 - 2 * h
-    line = me // LOW
-    bit_x = lax.rem(me, 2)
-    bit_y = lax.rem(me // 2, 2)
-    flip_x = 1 - 2 * bit_x
-    flip_y = 2 - 4 * bit_y
-    first = me + flip_x * (1 - h) + flip_y * h
-    second = me + flip_y * (1 - h) + flip_x * h
-    corner = me + flip_x + flip_y
-    has_down = line > 0
-    has_up = line < lines - 1
-
-    def piece(q, part):
-        return full_ref.at[pl.ds(q * depth + part * half, half)]
-
-    def copy(kind, q, brick, own=False):
-        src = slow_ref.at[pl.ds(h * half, half)] if own else piece(q, h)
-        return remote(src, piece(q, h), send_sem.at[kind, q], recv_sem.at[q], core, brick)
-
-    def twin_copy(q):
-        return remote(piece(q, h), piece(q, h), send_sem.at[4, q], twin_sem.at[q], twin, me)
-
-    barrier = pltpu.get_barrier_semaphore()
-
-    def greet(c, b):
-        pl.semaphore_signal(barrier, inc=1, device_id={"src": c, "brick": b}, device_id_type=MESH)
-
-    greet(twin, me)
-    greet(core, first)
-    greet(core, second)
-    pl.when(has_down)(lambda: greet(core, me - LOW))
-    pl.when(has_up)(lambda: greet(core, me + LOW))
-    pl.semaphore_wait(barrier, 3 + has_down.astype(jnp.int32) + has_up.astype(jnp.int32))
-
-    def sends(q, own, to_down, to_up, wait):
-        def go(c):
-            c.wait_send() if wait else c.start()
-
-        if to_down is not None:
-            pl.when(to_down)(lambda: go(copy(0, q, me - LOW, own)))
-        if to_up is not None:
-            pl.when(to_up)(lambda: go(copy(1, q, me + LOW, own)))
-        go(copy(2, q, first, own))
-        go(copy(3, q, second, own))
-
-    own_copy = pltpu.make_async_copy(slow_ref, full_ref.at[pl.ds(me * depth, depth)], own_sem)
-    sends(me, True, has_down, has_up, False)
-    own_copy.start()
-
-    def arrived(q):
-        remote(piece(q, h), piece(q, h), send_sem.at[0, q], recv_sem.at[q], core, first).wait_recv()
-
-    def on_line(base, i, act):
-        pl.when((i < lines) & (line >= i))(lambda: act(base - LOW * i, -1))
-        pl.when((i < lines) & (line + i < lines))(lambda: act(base + LOW * i, 1))
-
-    def both(base, i, act):
-        pl.when(i == 0)(lambda: act(base, 0))
-        pl.when(i > 0)(lambda: on_line(base, i, act))
-
-    def from_line(wait):
-        def act(q, side):
-            if not wait:
-                arrived(q)
-            sends(q, False, has_down if side > 0 else None, has_up if side < 0 else None, wait)
-            c = twin_copy(q)
-            c.wait_send() if wait else c.start()
-
-        return act
-
-    def from_first(wait):
-        def act(q, side):
-            if not wait:
-                arrived(q)
-            c = copy(3, q, second)
-            c.wait_send() if wait else c.start()
-            c = twin_copy(q)
-            c.wait_send() if wait else c.start()
-
-        return act
-
-    def from_second(wait):
-        def act(q, side):
-            if not wait:
-                arrived(q)
-            c = twin_copy(q)
-            c.wait_send() if wait else c.start()
-
-        return act
-
-    def turn(i, wait):
-        on_line(me, i, from_line(wait))
-        both(first, i - 1, from_first(wait))
-        both(second, i - 1, from_second(wait))
-        pl.when(i >= 2)(lambda: both(corner, i - 2, from_second(wait)))
-
-    @pl.loop(1, lines + 2)
-    def _(i):
-        turn(i, False)
-
-    own_copy.wait()
-    sends(me, True, has_down, has_up, True)
-
-    @pl.loop(1, lines + 2)
-    def _(i):
-        turn(i, True)
-
-    @pl.loop(0, bricks)
-    def _(q):
-        @pl.when(q != me)
-        def _():
-            remote(piece(q, 1 - h), piece(q, 1 - h), send_sem.at[4, q], twin_sem.at[q], twin, me).wait_recv()
-
-
 def window(pair_depth, grid_x, margin):
     length = min(grid_x, pair_depth + 2 * margin)
     pair = lax.axis_index("brick") // 2
     return jnp.clip(pair * pair_depth - margin, 0, grid_x - length), length
 
 
-def stations_kernel(grid_x, cells_y, pair_depth, stx_ref, sty_ref, stz_ref, obs_ref, cnt_ref, sum_ref, table):
+def stations(grid_x, cells_y, pair_depth, stx_ref, sty_ref, stz_ref, obs_ref, cnt_ref, sum_ref, table):
     rec = stx_ref.shape[1]
     cells_z = cnt_ref.shape[2]
     rows_y = cells_y // 8
@@ -178,8 +59,7 @@
     block = 256
     tiles = block // 8
 
-    @pl.loop(0, length * cells_y // block)
-    def _(step):
+    def tally(step):
         rows = lax.broadcasted_iota(jnp.int32, (block, rec), 0) + step * block
         pick = jnp.where(rows == row, 1.0, 0.0).astype(jnp.bfloat16)
         got = lax.dot_general(
@@ -190,6 +70,156 @@
             got[:, 2 * cells_z : 3 * cells_z] + got[:, 3 * cells_z :]
         )
         sum_ref[pl.ds(step * tiles, tiles)] = total.reshape(tiles, 8, cells_z)
+
+    return length * cells_y // block, tally
+
+
+def gather_kernel(
+    bricks,
+    pair_depth,
+    slow_ref,
+    stx_ref,
+    sty_ref,
+    stz_ref,
+    obs_ref,
+    full_ref,
+    cnt_ref,
+    sum_ref,
+    table,
+    send_sem,
+    recv_sem,
+    twin_sem,
+    own_sem,
+):
+    depth = slow_ref.shape[0]
+    half = depth // 2
+    lines = bricks // LOW
+    me = lax.axis_index("brick")
+    core = lax.axis_index("src")
+    h = lax.rem(core, 2)
+    twin = core + 1 - 2 * h
+    line = me // LOW
+    bit_x = lax.rem(me, 2)
+    bit_y = lax.rem(me // 2, 2)
+    flip_x = 1 - 2 * bit_x
+    flip_y = 2 - 4 * bit_y
+    first = me + flip_x * (1 - h) + flip_y * h
+    second = me + flip_y * (1 - h) + flip_x * h
+    corner = me + flip_x + flip_y
+    has_down = line > 0
+    has_up = line < lines - 1
+
+    def piece(q, part):
+        return full_ref.at[pl.ds(q * depth + part * half, half)]
+
+    def copy(kind, q, brick, own=False):
+        src = slow_ref.at[pl.ds(h * half, half)] if own else piece(q, h)
+        return remote(src, piece(q, h), send_sem.at[kind, q], recv_sem.at[q], core, brick)
+
+    def twin_copy(q):
+        return remote(piece(q, h), piece(q, h), send_sem.at[4, q], twin_sem.at[q], twin, me)
+
+    barrier = pltpu.get_barrier_semaphore()
+
+    def greet(c, b):
+        pl.semaphore_signal(barrier, inc=1, device_id={"src": c, "brick": b}, device_id_type=MESH)
+
+    greet(twin, me)
+    greet(core, first)
+    greet(core, second)
+    pl.when(has_down)(lambda: greet(core, me - LOW))
+    pl.when(has_up)(lambda: greet(core, me + LOW))
+    pl.semaphore_wait(barrier, 3 + has_down.astype(jnp.int32) + has_up.astype(jnp.int32))
+
+    def sends(q, own, to_down, to_up, wait):
+        def go(c):
+            c.wait_send() if wait else c.start()
+
+        if to_down is not None:
+            pl.when(to_down)(lambda: go(copy(0, q, me - LOW, own)))
+        if to_up is not None:
+            pl.when(to_up)(lambda: go(copy(1, q, me + LOW, own)))
+        go(copy(2, q, first, own))
+        go(copy(3, q, second, own))
+
+    own_copy = pltpu.make_async_copy(slow_ref, full_ref.at[pl.ds(me * depth, depth)], own_sem)
+    sends(me, True, has_down, has_up, False)
+    own_copy.start()
+
+    def arrived(q):
+        remote(piece(q, h), piece(q, h), send_sem.at[0, q], recv_sem.at[q], core, first).wait_recv()
+
+    def on_line(base, i, act):
+        pl.when((i < lines) & (line >= i))(lambda: act(base - LOW * i, -1))
+        pl.when((i < lines) & (line + i < lines))(lambda: act(base + LOW * i, 1))
+
+    def both(base, i, act):
+        pl.when(i == 0)(lambda: act(base, 0))
+        pl.when(i > 0)(lambda: on_line(base, i, act))
+
+    def from_line(wait):
+        def act(q, side):
+            if not wait:
+                arrived(q)
+            sends(q, False, has_down if side > 0 else None, has_up if side < 0 else None, wait)
+            c = twin_copy(q)
+            c.wait_send() if wait else c.start()
+
+        return act
+
+    def from_first(wait):
+        def act(q, side):
+            if not wait:
+                arrived(q)
+            c = copy(3, q, second)
+            c.wait_send() if wait else c.start()
+            c = twin_copy(q)
+            c.wait_send() if wait else c.start()
+
+        return act
+
+    def from_second(wait):
+        def act(q, side):
+            if not wait:
+                arrived(q)
+            c = twin_copy(q)
+            c.wait_send() if wait else c.start()
+
+        return act
+
+    def turn(i, wait):
+        on_line(me, i, from_line(wait))
+        both(first, i - 1, from_first(wait))
+        both(second, i - 1, from_second(wait))
+        pl.when(i >= 2)(lambda: both(corner, i - 2, from_second(wait)))
+
+    grid_x, cells_y, _ = full_ref.shape
+    blocks, tally = stations(
+        grid_x, cells_y, pair_depth, stx_ref, sty_ref, stz_ref, obs_ref, cnt_ref, sum_ref, table
+    )
+    share = -(-blocks // (lines + 1))
+
+    @pl.loop(1, lines + 2)
+    def _(i):
+        turn(i, False)
+
+        @pl.loop(0, share)
+        def _(j):
+            step = (i - 1) * share + j
+            pl.when(step < blocks)(lambda: tally(step))
+
+    own_copy.wait()
+    sends(me, True, has_down, has_up, True)
+
+    @pl.loop(1, lines + 2)
+    def _(i):
+        turn(i, True)
+
+    @pl.loop(0, bricks)
+    def _(q):
+        @pl.when(q != me)
+        def _():
+            remote(piece(q, 1 - h), piece(q, 1 - h), send_sem.at[4, q], twin_sem.at[q], twin, me).wait_recv()
 
 
 def solve_kernel(
@@ -224,6 +254,8 @@
     lane_last = lane == cells_z - 1
     sub_first = sub == 0
     sub_last = sub == 7
+    index_up = jnp.where(lane_last, cells_z - 2, lane + 1)
+    index_down = jnp.where(lane_first, 1, lane - 1)
 
     def layer_of(ref, x):
         return tuple(ref[x * rows + v] for v in range(rows))
@@ -264,7 +296,7 @@
             time[(grid_x + 1) * rows + v] = jnp.full((8, cells_z), value, jnp.float32)
 
     pads(big_value)
-    group = 2
+    group = FORWARD
 
     def forward(x, prev, cur):
         nxt = layer_of(time, x + 2)
@@ -276,8 +308,8 @@
                 up = jnp.where(sub_last, big_value, up)
             if v == 0:
                 down = jnp.where(sub_first, big_value, down)
-            ahead = jnp.where(lane_last, big_value, z_up(one))
-            behind = jnp.where(lane_first, big_value, z_down(one))
+            ahead = jnp.take_along_axis(one, index_up, axis=1)
+            behind = jnp.take_along_axis(one, index_down, axis=1)
             low = jnp.minimum(
                 jnp.minimum(jnp.minimum(prev[v], nxt[v]), jnp.minimum(up, down)), jnp.minimum(ahead, behind)
             )
@@ -358,12 +390,12 @@
 
     def weigh_body(i, carry):
         prev, cur = carry
-        for j in range(group):
-            nxt = weigh(base + i * group + j, prev, cur)
+        for j in range(2):
+            nxt = weigh(base + i * 2 + j, prev, cur)
             prev, cur = cur, nxt
         return prev, cur
 
-    lax.fori_loop(0, length // group, weigh_body, (layer_of(time, base), layer_of(time, base + 1)))
+    lax.fori_loop(0, length // 2, weigh_body, (layer_of(time, base), layer_of(time, base + 1)))
     for v in range(rows):
         field[v] = jnp.zeros((8, cells_z), jnp.float32)
         field[(length + 1) * rows + v] = jnp.zeros((8, cells_z), jnp.float32)
@@ -384,17 +416,17 @@
     @pl.loop(2, ITERS + 1)
     def _(sweep):
         margin = ITERS - sweep
-        span = jnp.minimum(grid_x, pair_depth + 2 * margin)
+        span = jnp.minimum(grid_x, (pair_depth + 2 * margin + BACKWARD - 1) // BACKWARD * BACKWARD)
         first = jnp.clip(pair * pair_depth - margin, 0, grid_x - span) - base
 
         def body(i, carry):
             prev, cur = carry
-            for j in range(group):
-                nxt = backward(first + i * group + j, prev, cur)
+            for j in range(BACKWARD):
+                nxt = backward(first + i * BACKWARD + j, prev, cur)
                 prev, cur = cur, nxt
             return prev, cur
 
-        lax.fori_loop(0, span // group, body, (layer_of(field, first), layer_of(field, first + 1)))
+        lax.fori_loop(0, span // BACKWARD, body, (layer_of(field, first), layer_of(field, first + 1)))
 
     mine = pair * pair_depth - base + 1
     for x in range(pair_depth):
@@ -458,31 +490,23 @@
     assert source_x.shape[0] == 2 and bricks % LOW == 0 and cores % 2 == 0
     f32 = jnp.float32
 
-    full = pl.pallas_call(
-        functools.partial(gather_kernel, bricks),
+    wide = min(grid_x, pair_depth + 2 * ITERS)
+    field = jax.ShapeDtypeStruct((wide * rows, 8, cells_z), f32)
+    full, cnt, total = pl.pallas_call(
+        functools.partial(gather_kernel, bricks, pair_depth),
         name="gather",
-        out_shape=jax.ShapeDtypeStruct((grid_x, cells_y, cells_z), f32),
-        in_specs=[VMEM],
-        out_specs=VMEM,
+        out_shape=(jax.ShapeDtypeStruct((grid_x, cells_y, cells_z), f32), field, field),
+        in_specs=[VMEM] * 5,
+        out_specs=(VMEM, VMEM, VMEM),
         scratch_shapes=[
+            pltpu.VMEM((4 * cells_z, rec), jnp.bfloat16),
             pltpu.SemaphoreType.DMA((5, bricks)),
             pltpu.SemaphoreType.DMA((bricks,)),
             pltpu.SemaphoreType.DMA((bricks,)),
             pltpu.SemaphoreType.DMA,
         ],
         compiler_params=pltpu.CompilerParams(collective_id=0, has_side_effects=True),
-    )(slowness)
-
-    wide = min(grid_x, pair_depth + 2 * ITERS)
-    field = jax.ShapeDtypeStruct((wide * rows, 8, cells_z), f32)
-    cnt, total = pl.pallas_call(
-        functools.partial(stations_kernel, grid_x, cells_y, pair_depth),
-        name="stations",
-        out_shape=(field, field),
-        in_specs=[VMEM] * 4,
-        out_specs=(VMEM, VMEM),
-        scratch_shapes=[pltpu.VMEM((4 * cells_z, rec), jnp.bfloat16)],
-    )(station_x[None], station_y[None], station_z[None], observed)
+    )(slowness, station_x[None], station_y[None], station_z[None], observed)
 
     length = min(grid_x, pair_depth + 2 * (ITERS - 1))
     share = rec // bricks

time: 126 us -> 85.7 us (0.68)
  Pallas kernels: 122 us -> 82.1 us
    pallas_call x1, Pallas kernels: 79.2 us -> 47.6 us  [per_device(): pl.pallas_call(functools.partial(solve_kernel, pair_depth), name='solve',...]
    pallas_call x2 -> x1, Pallas kernels: 35.3 us -> 27 us  [per_device(): pl.pallas_call(functools.partial(gather_kernel, bricks, pair_depth), name...]
where the time goes in v2:
time: 85.7 us; the launch traced here: 85.5 us
  Pallas kernels  82.1 us (96%)
  other arithmetic  1.48 us (2%)
  local copies, waits for them, and re-layouts  1.23 us (1%)
    pallas_call x1, Pallas kernels, per_device(): pl.pallas_call(functools.partial(solve_kernel, pair_depth), name='solve',...  47.6 us
    pallas_call x1, Pallas kernels, per_device(): pl.pallas_call(functools.partial(gather_kernel, bricks, pair_depth), name...  27 us
    pallas_call x1, Pallas kernels, per_device(): pl.pallas_call(functools.partial(reduce_kernel, cores), name='reduce', ou...  7.51 us

profile of v2, /device:TPU:0, one launch (start us, length us, event | category | flops | bytes accessed | tf_op | source)
XLA Modules:
  0.0 85.5 jit_solution(6102779494107211060)
XLA Ops:
  0.6 27.0 %gather.1 = (f32[64,64,128]{2,1,0:T(8,128)}, f32[320,8,128]{2,1,0:T(8,128)}, f32[320,8,128]{2,1,0:T(8,128)}) custom-call(f32[4,64,128]{2,1,0:T(8,128)} %slow_ref.1, s32[1,2048]{1,0:T(1,128)} %bitcast.4, s32[1,2048]{1,0:T(1,128)} %bitcast.5, s32[1,2048]{1,0:T(1,128)} %bitcast.6, f32[2,2048]{1,0:T(2,128)} %obs_ref.1), custom_call_target="tpu_custom_call" | custom-call | tf_op jit(solution)/shard_map/gather/pallas_call | solution.py:495
  27.6 0.0 copy-start
  27.6 47.6 %solve.1 = (f32[8,64,128]{2,1,0:T(8,128)}, f32[2,1,128]{2,1,0:T(1,128)}) custom-call(s32[2]{0:T(128)} %sx_ref.1, s32[2]{0:T(128)} %sy_ref.1, s32[2]{0:T(128)} %sz_ref.1, s32[2048]{0:T(1024)} %stx_ref.1, s32[2048]{0:T(1024)} %sty_ref.1, s32[2048]{0:T(1024)} %stz_ref.1, f32[64,64,128]{2,1,0:T(8,128)} %get-tuple-element.9.slow_ref, ...), custom_call_target="tpu_custom_call" | custom-call | tf_op jit(solution)/shard_map/solve/pallas_call | solution.py:513
  75.2 7.5 %reduce.1 = (f32[4,32,128]{2,1,0:T(8,128)}, f32[2,1,128]{2,1,0:T(1,128)}) custom-call(f32[8,64,128]{2,1,0:T(8,128)} %get-tuple-element.12.adj_ref, f32[2,1,128]{2,1,0:T(1,128)} %get-tuple-element.13.arr_ref), custom_call_target="tpu_custom_call" | custom-call | tf_op jit(solution)/shard_map/reduce/pallas_call | solution.py:533
  82.8 0.0 copy-done
  82.8 1.5 %dynamic-slice_multiply_fusion = f32[4,32,128]{2,1,0:T(8,128)} fusion(f32[4,32,128]{2,1,0:T(8,128)} %get-tuple-element.14, f32[4,64,128]{2,1,0:T(8,128)S(1)} %copy-done, s32[]{:T(128)S(6)} %select_n.3), kind=kLoop, calls=%fused_computation | loop fusion | flops 16384 | bytes 196612 | tf_op jit(solution)/shard_map/mul | solution.py:552
  84.2 1.2 %copy.11 = f32[2,128]{1,0:T(2,128)} copy(f32[2,128]{1,0:T(2,128)} %bitcast.7) | data formatting | bytes 2048
Async XLA Ops:
  27.6 55.1 %copy-start = (f32[4,64,128]{2,1,0:T(8,128)S(1)}, f32[4,64,128]{2,1,0:T(8,128)}, u32[]{:S(2)}) copy-start(f32[4,64,128]{2,1,0:T(8,128)} %slow_ref.1) | copy-start | bytes 393220

commit v3 on v2

--- a/solution.py
+++ b/solution.py
@@ -86,6 +86,7 @@
     cnt_ref,
     sum_ref,
     table,
+    line_sem,
     send_sem,
     recv_sem,
     twin_sem,
@@ -106,8 +107,6 @@
     first = me + flip_x * (1 - h) + flip_y * h
     second = me + flip_y * (1 - h) + flip_x * h
     corner = me + flip_x + flip_y
-    has_down = line > 0
-    has_up = line < lines - 1
 
     def piece(q, part):
         return full_ref.at[pl.ds(q * depth + part * half, half)]
@@ -117,7 +116,7 @@
         return remote(src, piece(q, h), send_sem.at[kind, q], recv_sem.at[q], core, brick)
 
     def twin_copy(q):
-        return remote(piece(q, h), piece(q, h), send_sem.at[4, q], twin_sem.at[q], twin, me)
+        return remote(piece(q, h), piece(q, h), send_sem.at[2, q], twin_sem.at[q], twin, me)
 
     barrier = pltpu.get_barrier_semaphore()
 
@@ -127,23 +126,35 @@
     greet(twin, me)
     greet(core, first)
     greet(core, second)
-    pl.when(has_down)(lambda: greet(core, me - LOW))
-    pl.when(has_up)(lambda: greet(core, me + LOW))
-    pl.semaphore_wait(barrier, 3 + has_down.astype(jnp.int32) + has_up.astype(jnp.int32))
-
-    def sends(q, own, to_down, to_up, wait):
-        def go(c):
+    for k in range(1, lines):
+        pl.when(line >= k)(lambda k=k: greet(core, me - LOW * k))
+        pl.when(line + k < lines)(lambda k=k: greet(core, me + LOW * k))
+    pl.semaphore_wait(barrier, lines + 2)
+
+    def along(k, up):
+        dst = piece(me, h)
+        src = slow_ref.at[pl.ds(h * half, half)]
+        brick = me + LOW * k if up else me - LOW * k
+        return remote(src, dst, line_sem.at[int(up), k], recv_sem.at[me], core, brick)
+
+    def own_line(k, wait):
+        def go(up):
+            c = along(k, up)
             c.wait_send() if wait else c.start()
 
-        if to_down is not None:
-            pl.when(to_down)(lambda: go(copy(0, q, me - LOW, own)))
-        if to_up is not None:
-            pl.when(to_up)(lambda: go(copy(1, q, me + LOW, own)))
-        go(copy(2, q, first, own))
-        go(copy(3, q, second, own))
+        pl.when(line >= k)(lambda: go(False))
+        pl.when(line + k < lines)(lambda: go(True))
+
+    def sends(q, own, wait):
+        for kind, brick in ((0, first), (1, second)):
+            c = copy(kind, q, brick, own)
+            c.wait_send() if wait else c.start()
 
     own_copy = pltpu.make_async_copy(slow_ref, full_ref.at[pl.ds(me * depth, depth)], own_sem)
-    sends(me, True, has_down, has_up, False)
+    for k in range(1, lines):
+        own_line(k, False)
+        if k == 1:
+            sends(me, True, False)
     own_copy.start()
 
     def arrived(q):
@@ -161,7 +172,7 @@
         def act(q, side):
             if not wait:
                 arrived(q)
-            sends(q, False, has_down if side > 0 else None, has_up if side < 0 else None, wait)
+            sends(q, False, wait)
             c = twin_copy(q)
             c.wait_send() if wait else c.start()
 
@@ -171,7 +182,7 @@
         def act(q, side):
             if not wait:
                 arrived(q)
-            c = copy(3, q, second)
+            c = copy(1, q, second)
             c.wait_send() if wait else c.start()
             c = twin_copy(q)
             c.wait_send() if wait else c.start()
@@ -209,7 +220,9 @@
             pl.when(step < blocks)(lambda: tally(step))
 
     own_copy.wait()
-    sends(me, True, has_down, has_up, True)
+    sends(me, True, True)
+    for k in range(1, lines):
+        own_line(k, True)
 
     @pl.loop(1, lines + 2)
     def _(i):
@@ -219,7 +232,7 @@
     def _(q):
         @pl.when(q != me)
         def _():
-            remote(piece(q, 1 - h), piece(q, 1 - h), send_sem.at[4, q], twin_sem.at[q], twin, me).wait_recv()
+            remote(piece(q, 1 - h), piece(q, 1 - h), send_sem.at[2, q], twin_sem.at[q], twin, me).wait_recv()
 
 
 def solve_kernel(
@@ -267,10 +280,10 @@
         return cur[v - 1] if v else pltpu.roll(cur[rows - 1], 1, 0)
 
     def z_up(one):
-        return pltpu.roll(one, cells_z - 1, 1)
+        return jnp.take_along_axis(one, index_up, axis=1)
 
     def z_down(one):
-        return pltpu.roll(one, 1, 1)
+        return jnp.take_along_axis(one, index_down, axis=1)
 
     sx = sx_ref[parity]
     sy = sy_ref[parity]
@@ -308,8 +321,8 @@
                 up = jnp.where(sub_last, big_value, up)
             if v == 0:
                 down = jnp.where(sub_first, big_value, down)
-            ahead = jnp.take_along_axis(one, index_up, axis=1)
-            behind = jnp.take_along_axis(one, index_down, axis=1)
+            ahead = z_up(one)
+            behind = z_down(one)
             low = jnp.minimum(
                 jnp.minimum(jnp.minimum(prev[v], nxt[v]), jnp.minimum(up, down)), jnp.minimum(ahead, behind)
             )
@@ -500,7 +513,8 @@
         out_specs=(VMEM, VMEM, VMEM),
         scratch_shapes=[
             pltpu.VMEM((4 * cells_z, rec), jnp.bfloat16),
-            pltpu.SemaphoreType.DMA((5, bricks)),
+            pltpu.SemaphoreType.DMA((2, bricks // LOW)),
+            pltpu.SemaphoreType.DMA((3, bricks)),
             pltpu.SemaphoreType.DMA((bricks,)),
             pltpu.SemaphoreType.DMA((bricks,)),
             pltpu.SemaphoreType.DMA,

time: 85.7 us -> 86 us (level)
  no operation moved by 1% of the time
where the time goes in v3:
time: 86 us; the launch traced here: 85.8 us
  Pallas kernels  82.4 us (96%)
  other arithmetic  1.48 us (2%)
  local copies, waits for them, and re-layouts  1.23 us (1%)
    pallas_call x1, Pallas kernels, per_device(): pl.pallas_call(functools.partial(solve_kernel, pair_depth), name='solve',...  48.2 us
    pallas_call x1, Pallas kernels, per_device(): pl.pallas_call(functools.partial(gather_kernel, bricks, pair_depth), name...  27.3 us
    pallas_call x1, Pallas kernels, per_device(): pl.pallas_call(functools.partial(reduce_kernel, cores), name='reduce', ou...  6.9 us

profile of v3, /device:TPU:0, one launch (start us, length us, event | category | flops | bytes accessed | tf_op | source)
XLA Modules:
  0.0 85.8 jit_solution(5797833902676663462)
XLA Ops:
  0.6 27.3 %gather.1 = (f32[64,64,128]{2,1,0:T(8,128)}, f32[320,8,128]{2,1,0:T(8,128)}, f32[320,8,128]{2,1,0:T(8,128)}) custom-call(f32[4,64,128]{2,1,0:T(8,128)} %slow_ref.1, s32[1,2048]{1,0:T(1,128)} %bitcast.4, s32[1,2048]{1,0:T(1,128)} %bitcast.5, s32[1,2048]{1,0:T(1,128)} %bitcast.6, f32[2,2048]{1,0:T(2,128)} %obs_ref.1), custom_call_target="tpu_custom_call" | custom-call | tf_op jit(solution)/shard_map/gather/pallas_call | solution.py:508
  27.9 0.0 copy-start
  28.0 48.2 %solve.1 = (f32[8,64,128]{2,1,0:T(8,128)}, f32[2,1,128]{2,1,0:T(1,128)}) custom-call(s32[2]{0:T(128)} %sx_ref.1, s32[2]{0:T(128)} %sy_ref.1, s32[2]{0:T(128)} %sz_ref.1, s32[2048]{0:T(1024)} %stx_ref.1, s32[2048]{0:T(1024)} %sty_ref.1, s32[2048]{0:T(1024)} %stz_ref.1, f32[64,64,128]{2,1,0:T(8,128)} %get-tuple-element.9.slow_ref, ...), custom_call_target="tpu_custom_call" | custom-call | tf_op jit(solution)/shard_map/solve/pallas_call | solution.py:527
  76.2 6.9 %reduce.1 = (f32[4,32,128]{2,1,0:T(8,128)}, f32[2,1,128]{2,1,0:T(1,128)}) custom-call(f32[8,64,128]{2,1,0:T(8,128)} %get-tuple-element.12.adj_ref, f32[2,1,128]{2,1,0:T(1,128)} %get-tuple-element.13.arr_ref), custom_call_target="tpu_custom_call" | custom-call | tf_op jit(solution)/shard_map/reduce/pallas_call | solution.py:547
  83.1 0.0 copy-done
  83.1 1.5 %dynamic-slice_multiply_fusion = f32[4,32,128]{2,1,0:T(8,128)} fusion(f32[4,32,128]{2,1,0:T(8,128)} %get-tuple-element.14, f32[4,64,128]{2,1,0:T(8,128)S(1)} %copy-done, s32[]{:T(128)S(6)} %select_n.3), kind=kLoop, calls=%fused_computation | loop fusion | flops 16384 | bytes 196612 | tf_op jit(solution)/shard_map/mul | solution.py:566
  84.6 1.2 %copy.11 = f32[2,128]{1,0:T(2,128)} copy(f32[2,128]{1,0:T(2,128)} %bitcast.7) | data formatting | bytes 2048
Async XLA Ops:
  27.9 55.2 %copy-start = (f32[4,64,128]{2,1,0:T(8,128)S(1)}, f32[4,64,128]{2,1,0:T(8,128)}, u32[]{:S(2)}) copy-start(f32[4,64,128]{2,1,0:T(8,128)} %slow_ref.1) | copy-start | bytes 393220

commit v4 on v3

--- a/solution.py
+++ b/solution.py
@@ -53,7 +53,8 @@
     rest = seen - hi
     mid = rest.astype(jnp.bfloat16).astype(jnp.float32)
     lo = rest - mid
-    hit = lax.broadcasted_iota(jnp.int32, (cells_z, rec), 0) == stz_ref[...]
+    stz = stz_ref[...]
+    hit = lax.broadcasted_iota(jnp.int32, (cells_z, rec), 0) == (stz & 1) * (cells_z // 2) + (stz >> 1)
     for part, value in enumerate((jnp.ones_like(seen), hi, mid, lo)):
         table[pl.ds(part * cells_z, cells_z), :] = jnp.where(hit, value, 0.0).astype(jnp.bfloat16)
     block = 256
@@ -249,6 +250,8 @@
     adj_ref,
     arr_ref,
     time,
+    ping,
+    pong,
     cost,
     picked,
     weight,
@@ -267,8 +270,12 @@
     lane_last = lane == cells_z - 1
     sub_first = sub == 0
     sub_last = sub == 7
-    index_up = jnp.where(lane_last, cells_z - 2, lane + 1)
-    index_down = jnp.where(lane_first, 1, lane - 1)
+    half_z = cells_z // 2
+    upper = lane >= half_z
+    index_up = jnp.where(lane_last, half_z - 1, jnp.where(upper, lane - half_z + 1, lane + half_z))
+    index_down = jnp.where(lane_first, half_z, jnp.where(upper, lane - half_z, lane + half_z - 1))
+    split = jnp.where(upper, (lane - half_z) * 2 + 1, lane * 2)
+    join = (lane & 1) * half_z + (lane >> 1)
 
     def layer_of(ref, x):
         return tuple(ref[x * rows + v] for v in range(rows))
@@ -285,67 +292,92 @@
     def z_down(one):
         return jnp.take_along_axis(one, index_down, axis=1)
 
+    def swap(a, b):
+        moved = pltpu.roll(jnp.where(upper, a, b), half_z, 1)
+        return jnp.where(upper, moved, a), jnp.where(upper, b, moved)
+
+    half_x = grid_x // 2
     sx = sx_ref[parity]
     sy = sy_ref[parity]
     sz = sz_ref[parity]
-    dz = (lane - sz).astype(jnp.float32)
+    shift_x = jnp.where(upper, half_x, 0) - sx
+    z_even = jnp.where(upper, lane - half_z, lane) * 2 - sz
     flat = []
-    for v in range(rows):
-        dy = (sub * rows + v - sy).astype(jnp.float32)
-        flat.append(dy * dy + dz * dz)
-
-    @pl.loop(0, grid_x)
+    for odd in range(2):
+        dz = (z_even + odd).astype(jnp.float32)
+        for v in range(rows):
+            dy = (sub * rows + v - sy).astype(jnp.float32)
+            flat.append(dy * dy + dz * dz)
+
+    def slot(x, odd, v):
+        return (x * 2 + odd) * rows + v
+
+    @pl.loop(0, half_x)
     def _(x):
-        dx = (x - sx).astype(jnp.float32)
+        dx = (x + shift_x).astype(jnp.float32)
+        dx = dx * dx
         for v in range(rows):
-            slow = slow_ref[x, pl.ds(v, 8, stride=rows), :]
-            start = (start_slowness * spacing) * jnp.sqrt(dx * dx + flat[v])
-            cost[x * rows + v] = (2.0 * half_step) * slow
-            time[(x + 1) * rows + v] = start + half_step * slow
-
-    def pads(value):
-        for v in range(rows):
-            time[v] = jnp.full((8, cells_z), value, jnp.float32)
-            time[(grid_x + 1) * rows + v] = jnp.full((8, cells_z), value, jnp.float32)
-
-    pads(big_value)
-    group = FORWARD
-
-    def forward(x, prev, cur):
-        nxt = layer_of(time, x + 2)
-        for v in range(rows):
-            one = cur[v]
-            up = y_up(cur, v)
-            down = y_down(cur, v)
-            if v + 1 == rows:
-                up = jnp.where(sub_last, big_value, up)
-            if v == 0:
-                down = jnp.where(sub_first, big_value, down)
-            ahead = z_up(one)
-            behind = z_down(one)
-            low = jnp.minimum(
-                jnp.minimum(jnp.minimum(prev[v], nxt[v]), jnp.minimum(up, down)), jnp.minimum(ahead, behind)
-            )
-            time[(x + 1) * rows + v] = jnp.minimum(one, low + cost[x * rows + v])
-        return nxt
-
-    @pl.loop(0, ITERS)
-    def _(sweep):
-        def body(i, carry):
-            prev, cur = carry
-            for j in range(group):
-                nxt = forward(i * group + j, prev, cur)
-                prev, cur = cur, nxt
-            return prev, cur
-
-        lax.fori_loop(0, grid_x // group, body, (layer_of(time, 0), layer_of(time, 1)))
-
-    @pl.loop(0, grid_x)
+            near = jnp.take_along_axis(slow_ref[x, pl.ds(v, 8, stride=rows), :], split, axis=1)
+            far = jnp.take_along_axis(slow_ref[x + half_x, pl.ds(v, 8, stride=rows), :], split, axis=1)
+            for odd, slow in enumerate(swap(near, far)):
+                start = (start_slowness * spacing) * jnp.sqrt(dx + flat[odd * rows + v])
+                cost[slot(x, odd, v)] = (2.0 * half_step) * slow
+                ping[slot(x + 1, odd, v)] = start + half_step * slow
+
+    inner = jnp.where(upper, lane - half_z, lane)
+    far_index = (
+        jnp.where(inner == 0, lane, lane - 1),
+        jnp.where(inner == half_z - 1, lane, lane + 1),
+    )
+
+    def sweep(src, dst):
+        for odd in range(2):
+            for v in range(rows):
+                first = pltpu.roll(src[slot(1, odd, v)], half_z, 1)
+                last = pltpu.roll(src[slot(half_x, odd, v)], half_z, 1)
+                src[slot(0, odd, v)] = jnp.where(upper, last, big_value)
+                src[slot(half_x + 1, odd, v)] = jnp.where(upper, big_value, first)
+
+        @pl.loop(0, half_x // FORWARD)
+        def _(i):
+            for j in range(FORWARD):
+                x = i * FORWARD + j
+                cur = [[src[slot(x + 1, odd, v)] for v in range(rows)] for odd in range(2)]
+                for v in range(rows):
+                    for odd in range(2):
+                        one = cur[odd][v]
+                        pair_z = cur[1 - odd][v]
+                        up = y_up(cur[odd], v)
+                        down = y_down(cur[odd], v)
+                        if v + 1 == rows:
+                            up = jnp.where(sub_last, big_value, up)
+                        if v == 0:
+                            down = jnp.where(sub_first, big_value, down)
+                        far_z = jnp.take_along_axis(pair_z, far_index[odd], axis=1)
+                        along_x = jnp.minimum(src[slot(x, odd, v)], src[slot(x + 2, odd, v)])
+                        low = jnp.minimum(
+                            jnp.minimum(along_x, jnp.minimum(up, down)), jnp.minimum(pair_z, far_z)
+                        )
+                        dst[slot(x + 1, odd, v)] = jnp.minimum(one, low + cost[slot(x, odd, v)])
+
+    assert ITERS % 2 == 0
+
+    @pl.loop(0, ITERS // 2)
+    def _(_step):
+        sweep(ping, pong)
+        sweep(pong, ping)
+
+    @pl.loop(0, half_x)
     def _(x):
         for v in range(rows):
-            time[(x + 1) * rows + v] = time[(x + 1) * rows + v] - 0.5 * cost[x * rows + v]
-
-    pads(-big_value)
+            even, odd = (ping[slot(x + 1, k, v)] - 0.5 * cost[slot(x, k, v)] for k in range(2))
+            near, far = swap(even, odd)
+            time[(x + 1) * rows + v] = near
+            time[(x + half_x + 1) * rows + v] = far
+
+    for v in range(rows):
+        time[v] = jnp.full((8, cells_z), -big_value, jnp.float32)
+        time[(grid_x + 1) * rows + v] = jnp.full((8, cells_z), -big_value, jnp.float32)
 
     count = picked.shape[0]
     line = lax.broadcasted_iota(jnp.int32, (1, cells_z), 1)
@@ -356,9 +388,10 @@
         for j in range(unroll):
             r = pair * count + i * unroll + j
             y = sty_ref[r]
+            z = stz_ref[r]
             at = (stx_ref[r] + 1) * rows + (y & (rows - 1))
             got = time[at, pl.ds(y >> shift, 1), :]
-            picked[pl.ds(i * unroll + j, 1), :] = jnp.where(line == stz_ref[r], got, 0.0)
+            picked[pl.ds(i * unroll + j, 1), :] = jnp.where(line == (z & 1) * half_z + (z >> 1), got, 0.0)
 
     arrived = jnp.sum(jnp.transpose(picked[...]), axis=0, keepdims=True)
     arr_ref[0] = arrived[:, : count // 2]
@@ -444,7 +477,9 @@
     mine = pair * pair_depth - base + 1
     for x in range(pair_depth):
         for v in range(rows):
-            adj_ref[x, pl.ds(v, 8, stride=rows), :] = field[(mine + x) * rows + v]
+            adj_ref[x, pl.ds(v, 8, stride=rows), :] = jnp.take_along_axis(
+                field[(mine + x) * rows + v], join, axis=1
+            )
 
 
 def reduce_kernel(cores, adj_ref, arr_ref, out_ref, got_ref, slots, send_sem, recv_sem, word_send, word_recv):
@@ -535,6 +570,8 @@
         out_specs=(VMEM, VMEM),
         scratch_shapes=[
             pltpu.VMEM(((grid_x + 2) * rows, 8, cells_z), f32),
+            pltpu.VMEM(((grid_x + 4) * rows, 8, cells_z), f32),
+            pltpu.VMEM(((grid_x + 4) * rows, 8, cells_z), f32),
             pltpu.VMEM((grid_x * rows, 8, cells_z), f32),
             pltpu.VMEM((2 * share, cells_z), f32),
             pltpu.VMEM((6, length * rows, 8, cells_z), f32),

time: 86 us -> 80.5 us (0.936)
  Pallas kernels: 82.4 us -> 76.9 us
    pallas_call x1, Pallas kernels: 48.2 us -> 42.6 us  [per_device(): pl.pallas_call(functools.partial(solve_kernel, pair_depth), name='solve',...]
where the time goes in v4:
time: 80.5 us; the launch traced here: 80.2 us
  Pallas kernels  76.9 us (96%)
  other arithmetic  1.48 us (2%)
  local copies, waits for them, and re-layouts  1.23 us (2%)
    pallas_call x1, Pallas kernels, per_device(): pl.pallas_call(functools.partial(solve_kernel, pair_depth), name='solve',...  42.6 us
    pallas_call x1, Pallas kernels, per_device(): pl.pallas_call(functools.partial(gather_kernel, bricks, pair_depth), name...  27.3 us
    pallas_call x1, Pallas kernels, per_device(): pl.pallas_call(functools.partial(reduce_kernel, cores), name='reduce', ou...  6.9 us

profile of v4, /device:TPU:0, one launch (start us, length us, event | category | flops | bytes accessed | tf_op | source)
XLA Modules:
  0.0 80.2 jit_solution(9508230411280016073)
XLA Ops:
  0.6 27.3 %gather.1 = (f32[64,64,128]{2,1,0:T(8,128)}, f32[320,8,128]{2,1,0:T(8,128)}, f32[320,8,128]{2,1,0:T(8,128)}) custom-call(f32[4,64,128]{2,1,0:T(8,128)} %slow_ref.1, s32[1,2048]{1,0:T(1,128)} %bitcast.4, s32[1,2048]{1,0:T(1,128)} %bitcast.5, s32[1,2048]{1,0:T(1,128)} %bitcast.6, f32[2,2048]{1,0:T(2,128)} %obs_ref.1), custom_call_target="tpu_custom_call" | custom-call | tf_op jit(solution)/shard_map/gather/pallas_call | solution.py:543
  27.9 0.0 copy-start
  28.0 42.6 %solve.1 = (f32[8,64,128]{2,1,0:T(8,128)}, f32[2,1,128]{2,1,0:T(1,128)}) custom-call(s32[2]{0:T(128)} %sx_ref.1, s32[2]{0:T(128)} %sy_ref.1, s32[2]{0:T(128)} %sz_ref.1, s32[2048]{0:T(1024)} %stx_ref.1, s32[2048]{0:T(1024)} %sty_ref.1, s32[2048]{0:T(1024)} %stz_ref.1, f32[64,64,128]{2,1,0:T(8,128)} %get-tuple-element.9.slow_ref, ...), custom_call_target="tpu_custom_call" | custom-call | tf_op jit(solution)/shard_map/solve/pallas_call | solution.py:562
  70.6 6.9 %reduce.1 = (f32[4,32,128]{2,1,0:T(8,128)}, f32[2,1,128]{2,1,0:T(1,128)}) custom-call(f32[8,64,128]{2,1,0:T(8,128)} %get-tuple-element.12.adj_ref, f32[2,1,128]{2,1,0:T(1,128)} %get-tuple-element.13.arr_ref), custom_call_target="tpu_custom_call" | custom-call | tf_op jit(solution)/shard_map/reduce/pallas_call | solution.py:584
  77.5 0.0 copy-done
  77.5 1.5 %dynamic-slice_multiply_fusion = f32[4,32,128]{2,1,0:T(8,128)} fusion(f32[4,32,128]{2,1,0:T(8,128)} %get-tuple-element.14, f32[4,64,128]{2,1,0:T(8,128)S(1)} %copy-done, s32[]{:T(128)S(6)} %select_n.3), kind=kLoop, calls=%fused_computation | loop fusion | flops 16384 | bytes 196612 | tf_op jit(solution)/shard_map/mul | solution.py:603
  79.0 1.2 %copy.11 = f32[2,128]{1,0:T(2,128)} copy(f32[2,128]{1,0:T(2,128)} %bitcast.7) | data formatting | bytes 2048
Async XLA Ops:
  27.9 49.6 %copy-start = (f32[4,64,128]{2,1,0:T(8,128)S(1)}, f32[4,64,128]{2,1,0:T(8,128)}, u32[]{:S(2)}) copy-start(f32[4,64,128]{2,1,0:T(8,128)} %slow_ref.1) | copy-start | bytes 393220

commit v5 on v4

--- a/solution.py
+++ b/solution.py
@@ -15,6 +15,9 @@
 half_step = 0.5 * spacing
 LOW = 4
 FORWARD = 8
+GATHER_VMEM = 24 << 20
+SOLVE_VMEM = 40 << 20
+REDUCE_VMEM = 8 << 20
 BACKWARD = 4
 
 VMEM = pl.BlockSpec(memory_space=pltpu.VMEM)
@@ -209,16 +212,17 @@
     blocks, tally = stations(
         grid_x, cells_y, pair_depth, stx_ref, sty_ref, stz_ref, obs_ref, cnt_ref, sum_ref, table
     )
-    share = -(-blocks // (lines + 1))
-
-    @pl.loop(1, lines + 2)
-    def _(i):
-        turn(i, False)
-
-        @pl.loop(0, share)
-        def _(j):
-            step = (i - 1) * share + j
-            pl.when(step < blocks)(lambda: tally(step))
+    early = 2
+    rounds = lines + 1
+
+    @pl.loop(0, early + rounds)
+    def _(step):
+        pl.when(step < blocks)(lambda: tally(step))
+        pl.when(step >= early)(lambda: turn(step - early + 1, False))
+
+    @pl.loop(early + rounds, max(blocks, early + rounds))
+    def _(step):
+        tally(step)
 
     own_copy.wait()
     sends(me, True, True)
@@ -554,7 +558,9 @@
             pltpu.SemaphoreType.DMA((bricks,)),
             pltpu.SemaphoreType.DMA,
         ],
-        compiler_params=pltpu.CompilerParams(collective_id=0, has_side_effects=True),
+        compiler_params=pltpu.CompilerParams(
+            collective_id=0, has_side_effects=True, vmem_limit_bytes=GATHER_VMEM
+        ),
     )(slowness, station_x[None], station_y[None], station_z[None], observed)
 
     length = min(grid_x, pair_depth + 2 * (ITERS - 1))
@@ -578,6 +584,7 @@
             pltpu.VMEM((length * rows, 8, cells_z), f32),
             pltpu.VMEM(((length + 2) * rows, 8, cells_z), f32),
         ],
+        compiler_params=pltpu.CompilerParams(vmem_limit_bytes=SOLVE_VMEM),
     )(source_x, source_y, source_z, station_x, station_y, station_z, full, cnt, total)
 
     keep = cells_y // cores
@@ -597,7 +604,9 @@
             pltpu.SemaphoreType.DMA,
             pltpu.SemaphoreType.DMA,
         ],
-        compiler_params=pltpu.CompilerParams(collective_id=1, has_side_effects=True),
+        compiler_params=pltpu.CompilerParams(
+            collective_id=1, has_side_effects=True, vmem_limit_bytes=REDUCE_VMEM
+        ),
     )(adj, arr)
     own = lax.dynamic_slice_in_dim(slowness, lax.axis_index("src") * keep, keep, axis=1)
     return own * summed, arrivals[:, 0]

time: 80.5 us -> 80.5 us (level)
  local copies, waits for them, and re-layouts: 1.23 us -> 8.32 us
  Pallas kernels: 76.9 us -> 70.3 us
  other arithmetic: 1.48 us -> 0.64 us
    unnamed x3 -> x25, local copies, waits for them, and re-layouts: 1.23 us -> 8.32 us
    pallas_call x1, Pallas kernels: 27.3 us -> 24.3 us  [per_device(): pl.pallas_call(functools.partial(gather_kernel, bricks, pair_depth), name...]
    pallas_call x1, Pallas kernels: 42.6 us -> 40.5 us  [per_device(): pl.pallas_call(functools.partial(solve_kernel, pair_depth), name='solve',...]
    pallas_call x1, Pallas kernels: 6.9 us -> 5.41 us  [per_device(): pl.pallas_call(functools.partial(reduce_kernel, cores), name='reduce', ou...]
    mul x1, other arithmetic: 1.48 us -> 0.64 us  [per_device(): return (own * summed, arrivals[:, 0])]
where the time goes in v5:
time: 80.5 us; the launch traced here: 79.9 us
  Pallas kernels  70.3 us (87%)
  local copies, waits for them, and re-layouts  8.32 us (10%)
    pallas_call x1, Pallas kernels, per_device(): pl.pallas_call(functools.partial(solve_kernel, pair_depth), name='solve',...  40.5 us
    pallas_call x1, Pallas kernels, per_device(): pl.pallas_call(functools.partial(gather_kernel, bricks, pair_depth), name...  24.3 us
    unnamed x25, local copies, waits for them, and re-layouts  8.32 us
    pallas_call x1, Pallas kernels, per_device(): pl.pallas_call(functools.partial(reduce_kernel, cores), name='reduce', ou...  5.41 us

profile of v5, /device:TPU:0, one launch (start us, length us, event | category | flops | bytes accessed | tf_op | source)
XLA Modules:
  0.0 79.9 jit_solution(11150976361267424374)
XLA Ops:
  0.6 0.0 copy-start
  0.6 0.9 %copy-done = f32[4,64,128]{2,1,0:T(8,128)S(1)} copy-done((f32[4,64,128]{2,1,0:T(8,128)S(1)}, f32[4,64,128]{2,1,0:T(8,128)}, u32[]{:S(2)}) %copy-start) | copy-done | bytes 131096
  1.5 0.0 copy-start.2
  1.5 0.7 copy-done.2
  2.2 0.0 copy-start.4
  2.2 0.7 copy-done.4
  2.9 0.0 copy-start.6
  2.9 0.7 copy-done.6
  3.6 0.0 copy-start.8
  3.6 0.7 copy-done.8
  4.3 24.3 %gather.1 = (f32[64,64,128]{2,1,0:T(8,128)S(1)}, f32[320,8,128]{2,1,0:T(8,128)S(1)}, f32[320,8,128]{2,1,0:T(8,128)S(1)}) custom-call(f32[4,64,128]{2,1,0:T(8,128)S(1)} %copy-done, s32[1,2048]{1,0:T(1,128)S(1)} %bitcast.4, s32[1,2048]{1,0:T(1,128)S(1)} %bitcast.5, s32[1,2048]{1,0:T(1,128)S(1)} %bitcast.6, f32[2,2048]{1,0:T(2,128)S(1)} %copy-done.8), custom_call_target="tpu_custom_call" | custom-call | tf_op jit(solution)/shard_map/gather/pallas_call | solution.py:547
  28.7 0.0 copy-start.3
  28.7 0.7 copy-done.3
  29.4 0.0 copy-start.5
  29.4 0.7 copy-done.5
  30.1 0.0 copy-start.7
  30.1 0.7 copy-done.7
  30.8 0.0 copy-start.9
  30.8 0.7 copy-done.9
  31.4 0.0 copy-start.10
  31.4 0.7 copy-done.10
  32.1 0.0 copy-start.11
  32.1 0.7 copy-done.11
  32.8 0.0 copy-start.1
  32.8 40.5 %solve.1 = (f32[8,64,128]{2,1,0:T(8,128)S(1)}, f32[2,1,128]{2,1,0:T(1,128)S(1)}) custom-call(s32[2]{0:T(128)S(1)} %copy-done.9, s32[2]{0:T(128)S(1)} %copy-done.10, s32[2]{0:T(128)S(1)} %copy-done.11, s32[2048]{0:T(1024)S(1)} %copy-done.3, s32[2048]{0:T(1024)S(1)} %copy-done.5, s32[2048]{0:T(1024)S(1)} %copy-done.7, ...), custom_call_target="tpu_custom_call" | custom-call | tf_op jit(solution)/shard_map/solve/pallas_call | solution.py:568
  73.3 5.4 %reduce.1 = (f32[4,32,128]{2,1,0:T(8,128)S(1)}, f32[2,1,128]{2,1,0:T(1,128)S(1)}) custom-call(f32[8,64,128]{2,1,0:T(8,128)S(1)} %get-tuple-element.12.adj_ref, f32[2,1,128]{2,1,0:T(1,128)S(1)} %get-tuple-element.13.arr_ref), custom_call_target="tpu_custom_call" | custom-call | tf_op jit(solution)/shard_map/reduce/pallas_call | solution.py:591
  78.7 0.0 copy-done.1
  78.7 0.6 dynamic-slice_multiply_fusion
  79.3 0.6 copy.11
Async XLA Ops:
  0.6 0.9 %copy-start = (f32[4,64,128]{2,1,0:T(8,128)S(1)}, f32[4,64,128]{2,1,0:T(8,128)}, u32[]{:S(2)}) copy-start(f32[4,64,128]{2,1,0:T(8,128)} %slow_ref.1) | copy-start | bytes 393220
  1.5 0.7 copy-start.2
  2.2 0.7 copy-start.4
  2.9 0.7 copy-start.6
  3.6 0.7 copy-start.8
  28.7 0.7 copy-start.3
  29.4 0.7 copy-start.5
  30.1 0.7 copy-start.7
  30.8 0.7 copy-start.9
  31.4 0.7 copy-start.10
  32.1 0.7 copy-start.11
  32.8 45.9 %copy-start.1 = (f32[4,64,128]{2,1,0:T(8,128)S(1)}, f32[4,64,128]{2,1,0:T(8,128)}, u32[]{:S(2)}) copy-start(f32[4,64,128]{2,1,0:T(8,128)} %slow_ref.1) | copy-start | bytes 393220

commit v6 on v5

--- a/solution.py
+++ b/solution.py
@@ -22,6 +22,7 @@
 
 VMEM = pl.BlockSpec(memory_space=pltpu.VMEM)
 SMEM = pl.BlockSpec(memory_space=pltpu.SMEM)
+HBM = pl.BlockSpec(memory_space=pltpu.HBM)
 MESH = pl.DeviceIdType.MESH
 
 
@@ -95,7 +96,20 @@
     recv_sem,
     twin_sem,
     own_sem,
+    stx_buf,
+    sty_buf,
+    stz_buf,
+    obs_buf,
+    in_sem,
 ):
+    loads = [
+        pltpu.make_async_copy(src, dst, in_sem.at[k])
+        for k, (src, dst) in enumerate(
+            ((stx_ref, stx_buf), (sty_ref, sty_buf), (stz_ref, stz_buf), (obs_ref, obs_buf))
+        )
+    ]
+    for load in loads:
+        load.start()
     depth = slow_ref.shape[0]
     half = depth // 2
     lines = bricks // LOW
@@ -209,8 +223,10 @@
         pl.when(i >= 2)(lambda: both(corner, i - 2, from_second(wait)))
 
     grid_x, cells_y, _ = full_ref.shape
+    for load in loads:
+        load.wait()
     blocks, tally = stations(
-        grid_x, cells_y, pair_depth, stx_ref, sty_ref, stz_ref, obs_ref, cnt_ref, sum_ref, table
+        grid_x, cells_y, pair_depth, stx_buf, sty_buf, stz_buf, obs_buf, cnt_ref, sum_ref, table
     )
     early = 2
     rounds = lines + 1
@@ -245,9 +261,9 @@
     sx_ref,
     sy_ref,
     sz_ref,
-    stx_ref,
-    sty_ref,
-    stz_ref,
+    stx_hbm,
+    sty_hbm,
+    stz_hbm,
     slow_ref,
     cnt_ref,
     sum_ref,
@@ -261,7 +277,17 @@
     weight,
     supply,
     field,
+    stx_ref,
+    sty_ref,
+    stz_ref,
+    in_sem,
 ):
+    loads = [
+        pltpu.make_async_copy(src, dst, in_sem.at[k])
+        for k, (src, dst) in enumerate(((stx_hbm, stx_ref), (sty_hbm, sty_ref), (stz_hbm, stz_ref)))
+    ]
+    for load in loads:
+        load.start()
     grid_x, cells_y, cells_z = slow_ref.shape
     rows = cells_y // 8
     shift = rows.bit_length() - 1
@@ -382,6 +408,9 @@
     for v in range(rows):
         time[v] = jnp.full((8, cells_z), -big_value, jnp.float32)
         time[(grid_x + 1) * rows + v] = jnp.full((8, cells_z), -big_value, jnp.float32)
+
+    for load in loads:
+        load.wait()
 
     count = picked.shape[0]
     line = lax.broadcasted_iota(jnp.int32, (1, cells_z), 1)
@@ -548,7 +577,7 @@
         functools.partial(gather_kernel, bricks, pair_depth),
         name="gather",
         out_shape=(jax.ShapeDtypeStruct((grid_x, cells_y, cells_z), f32), field, field),
-        in_specs=[VMEM] * 5,
+        in_specs=[VMEM] + [HBM] * 4,
         out_specs=(VMEM, VMEM, VMEM),
         scratch_shapes=[
             pltpu.VMEM((4 * cells_z, rec), jnp.bfloat16),
@@ -557,6 +586,11 @@
             pltpu.SemaphoreType.DMA((bricks,)),
             pltpu.SemaphoreType.DMA((bricks,)),
             pltpu.SemaphoreType.DMA,
+            pltpu.VMEM((1, rec), jnp.int32),
+            pltpu.VMEM((1, rec), jnp.int32),
+            pltpu.VMEM((1, rec), jnp.int32),
+            pltpu.VMEM(observed.shape, f32),
+            pltpu.SemaphoreType.DMA((4,)),
         ],
         compiler_params=pltpu.CompilerParams(
             collective_id=0, has_side_effects=True, vmem_limit_bytes=GATHER_VMEM
@@ -572,7 +606,7 @@
             jax.ShapeDtypeStruct((pair_depth, cells_y, cells_z), f32),
             jax.ShapeDtypeStruct((2, 1, share), f32),
         ),
-        in_specs=[SMEM] * 6 + [VMEM] * 3,
+        in_specs=[SMEM] * 3 + [HBM] * 3 + [VMEM] * 3,
         out_specs=(VMEM, VMEM),
         scratch_shapes=[
             pltpu.VMEM(((grid_x + 2) * rows, 8, cells_z), f32),
@@ -583,6 +617,10 @@
             pltpu.VMEM((6, length * rows, 8, cells_z), f32),
             pltpu.VMEM((length * rows, 8, cells_z), f32),
             pltpu.VMEM(((length + 2) * rows, 8, cells_z), f32),
+            pltpu.SMEM((rec,), jnp.int32),
+            pltpu.SMEM((rec,), jnp.int32),
+            pltpu.SMEM((rec,), jnp.int32),
+            pltpu.SemaphoreType.DMA((3,)),
         ],
         compiler_params=pltpu.CompilerParams(vmem_limit_bytes=SOLVE_VMEM),
     )(source_x, source_y, source_z, station_x, station_y, station_z, full, cnt, total)

time: 80.5 us -> 80.4 us (level)
  no operation moved by 1% of the time
where the time goes in v6:
time: 80.4 us; the launch traced here: 79.8 us
  Pallas kernels  70.1 us (87%)
  local copies, waits for them, and re-layouts  8.32 us (10%)
    pallas_call x1, Pallas kernels, per_device(): pl.pallas_call(functools.partial(solve_kernel, pair_depth), name='solve',...  40.2 us
    pallas_call x1, Pallas kernels, per_device(): pl.pallas_call(functools.partial(gather_kernel, bricks, pair_depth), name...  24.5 us
    unnamed x25, local copies, waits for them, and re-layouts  8.32 us
    pallas_call x1, Pallas kernels, per_device(): pl.pallas_call(functools.partial(reduce_kernel, cores), name='reduce', ou...  5.41 us

profile of v6, /device:TPU:0, one launch (start us, length us, event | category | flops | bytes accessed | tf_op | source)
XLA Modules:
  0.0 79.8 jit_solution(13356869540199301322)
XLA Ops:
  0.6 0.0 copy-start
  0.6 0.9 %copy-done = f32[4,64,128]{2,1,0:T(8,128)S(1)} copy-done((f32[4,64,128]{2,1,0:T(8,128)S(1)}, f32[4,64,128]{2,1,0:T(8,128)}, u32[]{:S(2)}) %copy-start) | copy-done | bytes 131096
  1.5 0.0 copy-start.2
  1.5 0.7 copy-done.2
  2.2 0.0 copy-start.4
  2.2 0.7 copy-done.4
  2.9 0.0 copy-start.6
  2.9 0.7 copy-done.6
  3.6 0.0 copy-start.8
  3.6 0.7 copy-done.8
  4.3 24.5 %gather.1 = (f32[64,64,128]{2,1,0:T(8,128)S(1)}, f32[320,8,128]{2,1,0:T(8,128)S(1)}, f32[320,8,128]{2,1,0:T(8,128)S(1)}) custom-call(f32[4,64,128]{2,1,0:T(8,128)S(1)} %copy-done, s32[1,2048]{1,0:T(1,128)S(1)} %bitcast.4, s32[1,2048]{1,0:T(1,128)S(1)} %bitcast.5, s32[1,2048]{1,0:T(1,128)S(1)} %bitcast.6, f32[2,2048]{1,0:T(2,128)S(1)} %copy-done.8), custom_call_target="tpu_custom_call" | custom-call | tf_op jit(solution)/shard_map/gather/pallas_call | solution.py:576
  28.9 0.0 copy-start.3
  28.9 0.7 copy-done.3
  29.6 0.0 copy-start.5
  29.6 0.7 copy-done.5
  30.3 0.0 copy-start.7
  30.3 0.7 copy-done.7
  31.0 0.0 copy-start.9
  31.0 0.7 copy-done.9
  31.6 0.0 copy-start.10
  31.6 0.7 copy-done.10
  32.3 0.0 copy-start.11
  32.3 0.7 copy-done.11
  33.0 0.0 copy-start.1
  33.0 40.2 %solve.1 = (f32[8,64,128]{2,1,0:T(8,128)S(1)}, f32[2,1,128]{2,1,0:T(1,128)S(1)}) custom-call(s32[2]{0:T(128)S(1)} %copy-done.9, s32[2]{0:T(128)S(1)} %copy-done.10, s32[2]{0:T(128)S(1)} %copy-done.11, s32[2048]{0:T(1024)S(1)} %copy-done.3, s32[2048]{0:T(1024)S(1)} %copy-done.5, s32[2048]{0:T(1024)S(1)} %copy-done.7, ...), custom_call_target="tpu_custom_call" | custom-call | tf_op jit(solution)/shard_map/solve/pallas_call | solution.py:602
  73.2 5.4 %reduce.1 = (f32[4,32,128]{2,1,0:T(8,128)S(1)}, f32[2,1,128]{2,1,0:T(1,128)S(1)}) custom-call(f32[8,64,128]{2,1,0:T(8,128)S(1)} %get-tuple-element.12.adj_ref, f32[2,1,128]{2,1,0:T(1,128)S(1)} %get-tuple-element.13.arr_ref), custom_call_target="tpu_custom_call" | custom-call | tf_op jit(solution)/shard_map/reduce/pallas_call | solution.py:629
  78.6 0.0 copy-done.1
  78.6 0.6 dynamic-slice_multiply_fusion
  79.2 0.6 copy.11
Async XLA Ops:
  0.6 0.9 %copy-start = (f32[4,64,128]{2,1,0:T(8,128)S(1)}, f32[4,64,128]{2,1,0:T(8,128)}, u32[]{:S(2)}) copy-start(f32[4,64,128]{2,1,0:T(8,128)} %slow_ref.1) | copy-start | bytes 393220
  1.5 0.7 copy-start.2
  2.2 0.7 copy-start.4
  2.9 0.7 copy-start.6
  3.6 0.7 copy-start.8
  28.9 0.7 copy-start.3
  29.6 0.7 copy-start.5
  30.3 0.7 copy-start.7
  31.0 0.7 copy-start.9
  31.6 0.7 copy-start.10
  32.3 0.7 copy-start.11
  33.0 45.6 %copy-start.1 = (f32[4,64,128]{2,1,0:T(8,128)S(1)}, f32[4,64,128]{2,1,0:T(8,128)}, u32[]{:S(2)}) copy-start(f32[4,64,128]{2,1,0:T(8,128)} %slow_ref.1) | copy-start | bytes 393220
